TPU v7x, 32 devices: a whole 2x2x4 slice. The times are simulated.
32 devices in a mesh: groups: 2 (over x), ctx: 16 (over z, y, core).
Axes of the slice: x: 2, y: 2, z: 4, core: 2. Of those that a mesh axis runs over, the one named last changes fastest.
Arguments:
- queries: bfloat16 [8192, 2048], P(('groups', 'ctx')), parts along dimension 0, may hold values from -14 to 14
- keys: bfloat16 [8192, 512], P(('groups', 'ctx')), parts along dimension 0, may hold values from -6 to 6
- values: bfloat16 [8192, 512], P(('groups', 'ctx')), parts along dimension 0, may hold values from -6 to 6
- doc_starts: int32 [32, 2], P(('groups', 'ctx')), parts along dimension 0, may hold values from -1 to 31, as said below
Outputs:
- attended: bfloat16 [8192, 2048], P(('groups', 'ctx')), parts along dimension 0
There are 2 independent parts, one for each index of `groups`. A program takes and returns all parts, laid end to end along the dimension named above; each array names one. Nothing has to cross between parts.
Inputs may be any that keep to these rules, and one draw needn't show every extreme that they name: `doc_starts`: row c lists, rising, the global indices of the blocks of 128 tokens in tokens c * 256 .. (c + 1) * 256 - 1 at which a document begins, then -1 in the remaining slots. The first document begins in row 0 after block 0; no document begins in row 1; a document begins at the last block.
All inputs are finite; a program needn't handle non-finite values.
Results may differ from a plain program's by a relative error of at most 0.0032.
Values may be sent and summed in bfloat16 or wider, within the bound.
No kernel may reach another device: no remote copies, remote signals or barrier semaphores. Data moves between devices by JAX's collectives and lax.ppermute only.
A program may use at most 64 MiB of HBM per device.

v0:
```python
import functools
import math

import jax
import jax.numpy as jnp
from jax import lax
from jax.experimental import pallas as pl
from jax.experimental.pallas import tpu as pltpu
from jax.sharding import PartitionSpec as P

HD = 128
WINDOW = 2048
BLK = 128
LEN = 256
GROUP = 4
WIDE = GROUP * LEN
INFO = 2 * LEN
CHUNK = (INFO + 16, LEN)
MASKED = -1e30
COEF = math.log2(math.e) / math.sqrt(HD)

VMEM = pl.BlockSpec(memory_space=pltpu.VMEM)
SMEM = pl.BlockSpec(memory_space=pltpu.SMEM)
ANY = pl.BlockSpec(memory_space=pl.ANY)
LIMIT = 20 << 20


def exchanged(x, bit):
    n = lax.axis_size("ctx")
    return lax.ppermute(x, "ctx", [(i, i ^ bit) for i in range(n)])


def shifted(x, distance):
    n = lax.axis_size("ctx")
    return lax.ppermute(x, "ctx", [(i, (i + distance) % n) for i in range(n)])


def my_half(other):
    core = lax.rem(lax.axis_index("ctx"), 2)
    return 1 - core if other else core


def columns(index, width):
    return pl.ds(pl.multiple_of(index * width, width), width)


def prep_kv_kernel(other, k_ref, v_ref, *refs):
    *tables, out_ref, k_buf, v_buf, sems = refs
    pick = my_half(other)
    copies = [
        pltpu.make_async_copy(ref.at[:, columns(pick, 2 * HD)], buf, sems.at[i])
        for i, (ref, buf) in enumerate(((k_ref, k_buf), (v_ref, v_buf)))
    ]
    for copy in copies:
        copy.start()
    lane = lax.broadcasted_iota(jnp.int32, (16, LEN), 1)
    info = jnp.full((16, LEN), -1, jnp.int32)
    slot = 0
    for table in tables:
        for col in range(2):
            info = jnp.where(lane == slot, table[0, col], info)
            slot += 1
    out_ref[INFO:, :] = info.astype(jnp.float32).astype(jnp.bfloat16)
    copies[1].wait()
    for pair in range(2):
        out_ref[LEN + pair * HD : LEN + (pair + 1) * HD, :] = v_buf[:, pair * HD : (pair + 1) * HD].T
    copies[0].wait()
    out_ref[:LEN, :] = k_buf[...]


def prep_kv(keys, values, tables, other):
    return pl.pallas_call(
        functools.partial(prep_kv_kernel, other),
        out_shape=jax.ShapeDtypeStruct(CHUNK, jnp.bfloat16),
        in_specs=[ANY, ANY] + [SMEM] * len(tables),
        out_specs=VMEM,
        scratch_shapes=[pltpu.VMEM((LEN, LEN), jnp.bfloat16)] * 2 + [pltpu.SemaphoreType.DMA((2,))],
        compiler_params=pltpu.CompilerParams(vmem_limit_bytes=4 << 20 if other else None),
        name="prep_kv",
    )(keys, values, *tables)


def prep_q_kernel(other, q_ref, out_ref, q_buf, sems):
    pick = my_half(other)
    pairs = out_ref.shape[0]
    copies = [
        pltpu.make_async_copy(
            q_ref.at[:, columns(pick * pairs + pair, GROUP * HD)], q_buf.at[pair], sems.at[pair]
        )
        for pair in range(pairs)
    ]
    for copy in copies:
        copy.start()
    for pair, copy in enumerate(copies):
        copy.wait()
        for head in range(GROUP):
            out_ref[pair, :, head * LEN : (head + 1) * LEN] = q_buf[
                pair, :, head * HD : (head + 1) * HD
            ].T


def prep_q(queries, other):
    pairs = queries.shape[1] // (2 * GROUP * HD)
    return pl.pallas_call(
        functools.partial(prep_q_kernel, other),
        out_shape=jax.ShapeDtypeStruct((pairs, HD, WIDE), jnp.bfloat16),
        in_specs=[ANY],
        out_specs=VMEM,
        scratch_shapes=[
            pltpu.VMEM((pairs, LEN, GROUP * HD), jnp.bfloat16),
            pltpu.SemaphoreType.DMA((pairs,)),
        ],
        compiler_params=pltpu.CompilerParams(vmem_limit_bytes=4 << 20),
        name="prep_q",
    )(queries)


def pick_kernel(lower_ref, upper_ref, out_ref, sem):
    second = lax.rem(lax.div(lax.axis_index("ctx"), 2), 2) == 1

    @pl.when(second)
    def _():
        pltpu.make_async_copy(upper_ref, out_ref, sem).start()

    @pl.when(jnp.logical_not(second))
    def _():
        pltpu.make_async_copy(lower_ref, out_ref, sem).start()

    pltpu.make_async_copy(lower_ref, out_ref, sem).wait()


def crossed(lower, upper):
    picked = pl.pallas_call(
        pick_kernel,
        out_shape=jax.ShapeDtypeStruct(lower.shape, lower.dtype),
        in_specs=[ANY] * 2,
        out_specs=VMEM,
        scratch_shapes=[pltpu.SemaphoreType.DMA],
        compiler_params=pltpu.CompilerParams(vmem_limit_bytes=2 << 20),
        name="pick",
    )(lower, upper)
    return exchanged(picked, 2)


def merge_kernel(got_ref, full_in, full_ref, sem):
    copy = pltpu.make_async_copy(got_ref, full_ref.at[:, columns(my_half(True), got_ref.shape[1])], sem)
    copy.start()
    copy.wait()


def merge(got, full):
    return pl.pallas_call(
        merge_kernel,
        out_shape=jax.ShapeDtypeStruct(full.shape, full.dtype),
        in_specs=[VMEM, ANY],
        out_specs=ANY,
        scratch_shapes=[pltpu.SemaphoreType.DMA],
        input_output_aliases={1: 0},
        compiler_params=pltpu.CompilerParams(vmem_limit_bytes=4 << 20),
        name="merge",
    )(got, full)


def pair_step(q_ref, chunk_ref, acc_ref, ml_ref, chunk, tile, pair, bounds):
    k_tile = chunk_ref[chunk, :LEN, pl.ds(pl.multiple_of(pair * HD, HD), HD)]
    v_turned = chunk_ref[chunk, pl.ds(pl.multiple_of(LEN + pair * HD, HD), HD), :]
    queries = q_ref[tile, pair]
    peaks = ml_ref[tile, pair, 0]
    totals = ml_ref[tile, pair, 1]
    lanes = [slice(head * LEN, (head + 1) * LEN) for head in range(GROUP)]
    scores = [
        jnp.dot(k_tile, queries[:, at], preferred_element_type=jnp.float32) for at in lanes
    ]
    if bounds is not None:
        scores = [jnp.where(bounds, s, MASKED) for s in scores]
    new = [
        jnp.maximum(peaks[:, at], jnp.max(s, axis=0, keepdims=True)) for at, s in zip(lanes, scores)
    ]
    weights = [jnp.exp2((s - peak) * COEF) for s, peak in zip(scores, new)]
    products = [
        jnp.dot(v_turned, w.astype(jnp.bfloat16), preferred_element_type=jnp.float32) for w in weights
    ]
    fades = [jnp.exp2((peaks[:, at] - peak) * COEF) for at, peak in zip(lanes, new)]
    sums = [jnp.sum(w, axis=0, keepdims=True) for w in weights]
    for head, at in enumerate(lanes):
        ml_ref[tile, pair, 0, :, at] = new[head]
        ml_ref[tile, pair, 1, :, at] = totals[:, at] * fades[head] + sums[head]
        acc_ref[tile, pair, :, at] = acc_ref[tile, pair, :, at] * fades[head] + products[head]


def attend_kernel(sources, n_infos, first, last, *refs):
    refs = list(refs)
    take = lambda n: [refs.pop(0) for _ in range(n)]
    count = len(sources)
    info_in = take(n_infos)
    q_in = take(2)
    chunk_in = take(count)
    state_in = [] if first else take(3)
    outs = take(2 if last else 3)
    q_ref, chunk_ref, info_ref = take(3)
    state = acc_ref, ml_ref, best_ref = take(3)
    buffers = take(2) if last else []
    info_sem, q_sem, chunk_sem, state_sem = take(4)
    stretch = lax.axis_index("ctx")
    pairs = acc_ref.shape[1]

    copy_of = pltpu.make_async_copy
    info_copies = [
        copy_of(ref.at[INFO:, :], info_ref.at[i], info_sem.at[i]) for i, ref in enumerate(info_in)
    ]
    state_copies = [
        copy_of(source, target, state_sem.at[i]) for i, (source, target) in enumerate(zip(state_in, state))
    ]
    bulk = [copy_of(q_in[i], q_ref.at[i], q_sem.at[i]) for i in range(2)]
    bulk += [copy_of(chunk_in[i], chunk_ref.at[i], chunk_sem.at[i]) for i in range(count)]
    for copy in info_copies + state_copies[::-1] + bulk:
        copy.start()
    if first:
        acc_ref[...] = jnp.zeros_like(acc_ref)
        ml_ref[:, :, 0] = jnp.full_like(ml_ref[:, :, 0], MASKED)
        ml_ref[:, :, 1] = jnp.zeros_like(ml_ref[:, :, 1])
        best_ref[...] = jnp.full_like(best_ref, -1.0)

    for copy in info_copies + state_copies[2:]:
        copy.wait()
    low, high = [], []
    for tile in range(2):
        for block, found in ((0, low), (1, high)):
            row = 2 * tile + block
            number = (2 * (stretch ^ tile) + block).astype(jnp.float32)
            best = best_ref[row]
            for i in range(n_infos):
                entries = info_ref[i, 0:1, :HD].astype(jnp.float32)
                best = jnp.maximum(best, jnp.where(entries <= number, entries, -1.0))
            best_ref[row] = best
            found.append(jnp.max(best).astype(jnp.int32))

    second = lax.rem(lax.div(stretch, 2), 2) == 1
    source_of = [
        (stretch ^ bits) - jnp.where(second, upper, lower) for bits, lower, upper in sources
    ]

    def view(source, tile, low_start, high_start):
        where = stretch ^ tile
        first_key, first_query = source * LEN, where * LEN
        low_limit = jnp.maximum(low_start * BLK, first_query - WINDOW + 1)
        seen = (source >= 0) & (source <= where) & (first_key + LEN > low_limit)
        high_limit = jnp.maximum(high_start * BLK, first_query + LEN - WINDOW)
        whole = (source < where) & (first_key >= high_limit)
        return seen, whole

    busy = functools.reduce(
        jnp.logical_or,
        [view(source, tile, low[tile], high[tile])[0] for source in source_of for tile in range(2)],
    )
    for copy in state_copies[:2] + bulk:
        copy.wait()

    def visit(step, _):
        chunk, tile = lax.div(step, 2), lax.rem(step, 2)
        source = source_of[0]
        for i in range(1, count):
            source = jnp.where(chunk == i, source_of[i], source)
        low_start = jnp.where(tile == 0, low[0], low[1])
        high_start = jnp.where(tile == 0, high[0], high[1])
        seen, whole = view(source, tile, low_start, high_start)

        def all_heads(masked):
            bounds = None
            if masked:
                lane = lax.broadcasted_iota(jnp.int32, (1, LEN), 1)
                query_pos = (stretch ^ tile) * LEN + lane
                start = jnp.where(lane < BLK, low_start, high_start) * BLK
                least = jnp.maximum(start, query_pos - (WINDOW - 1))
                key_pos = source * LEN + lax.broadcasted_iota(jnp.int32, (LEN, LEN), 0)
                bounds = (key_pos <= query_pos) & (key_pos >= least)

            def one_pair(pair, _):
                pair_step(q_ref, chunk_ref, acc_ref, ml_ref, chunk, tile, pair, bounds)
                return 0

            lax.fori_loop(0, pairs, one_pair, 0)

        @pl.when(seen & whole)
        def _():
            all_heads(False)

        @pl.when(seen & jnp.logical_not(whole))
        def _():
            all_heads(True)

        return 0

    @pl.when(busy)
    def _():
        lax.fori_loop(0, 2 * count, visit, 0)

    if not last:
        back = [
            copy_of(source, target, state_sem.at[i]) for i, (source, target) in enumerate(zip(state, outs))
        ]
        back[2].start()

        @pl.when(busy | first)
        def _():
            for copy in back[:2]:
                copy.start()
            for copy in back[:2]:
                copy.wait()

        back[2].wait()
        return

    sinks = (outs[0].at[:, columns(my_half(False), outs[1].shape[1])], outs[1])
    leaving = []
    for tile in (1, 0):
        lane = lax.broadcasted_iota(jnp.int32, (1, WIDE), 1)
        start = jnp.where(lax.rem(lane, LEN) < BLK, low[tile], high[tile])
        active = (start >= 0) | ((stretch ^ tile) >= 1)
        for pair in range(pairs):
            scale = jnp.where(active, 1.0 / ml_ref[tile, pair, 1], 0.0)
            for head in range(GROUP):
                lanes = slice(head * LEN, (head + 1) * LEN)
                blended = (acc_ref[tile, pair, :, lanes] * scale[:, lanes]).astype(jnp.bfloat16)
                at = (pair * GROUP + head) * HD
                buffers[tile][:, at : at + HD] = blended.T
        copy = copy_of(buffers[tile], sinks[tile], q_sem.at[tile])
        copy.start()
        leaving.append(copy)
    for copy in leaving:
        copy.wait()


def attend(infos, qs, chunks, sources, state, width=0):
    last = width > 0
    first = state is None
    pairs = qs[0].shape[0]
    args = list(infos) + list(qs) + list(chunks)
    state_shapes = (2, pairs, HD, WIDE), (2, pairs, 2, 1, WIDE), (4, 1, HD)
    aliases = {}
    if not first:
        if not last:
            aliases = {len(args) + i: i for i in range(3)}
        args += list(state)
    scratch = [
        pltpu.VMEM((2,) + qs[0].shape, jnp.bfloat16),
        pltpu.VMEM((len(chunks),) + CHUNK, jnp.bfloat16),
        pltpu.VMEM((max(len(infos), 1), 16, LEN), jnp.bfloat16),
    ] + [pltpu.VMEM(s, jnp.float32) for s in state_shapes]
    if last:
        half = pairs * GROUP * HD
        shapes = [jax.ShapeDtypeStruct((LEN, w), jnp.bfloat16) for w in (width, half)]
        scratch += [pltpu.VMEM((LEN, half), jnp.bfloat16)] * 2
    else:
        shapes = [jax.ShapeDtypeStruct(s, jnp.float32) for s in state_shapes]
    scratch += [pltpu.SemaphoreType.DMA((n,)) for n in (max(len(infos), 1), 2, len(chunks), 3)]
    elements = len(chunks) * 2 * pairs * LEN * WIDE
    return pl.pallas_call(
        functools.partial(attend_kernel, sources, len(infos), first, last),
        out_shape=shapes,
        in_specs=[ANY] * len(args),
        out_specs=[ANY] * len(shapes),
        scratch_shapes=scratch,
        input_output_aliases=aliases,
        cost_estimate=pl.CostEstimate(
            flops=4 * HD * elements, bytes_accessed=6 << 20, transcendentals=elements
        ),
        compiler_params=pltpu.CompilerParams(vmem_limit_bytes=LIMIT),
        name="attend",
    )(*args)


def steps(queries, keys, values, doc_starts):
    rows, width = queries.shape
    assert rows == LEN and keys.shape[1] == 4 * HD and lax.axis_size("ctx") % 4 == 0
    own = prep_kv(keys, values, (doc_starts,), False)
    a_own = shifted(own, 4)
    across = exchanged(doc_starts, 2)
    q_send = prep_q(queries, True)
    q_pair = exchanged(q_send, 1)
    send = prep_kv(keys, values, (doc_starts, across), True)
    pair = exchanged(send, 1)
    qs = (prep_q(queries, False), q_pair)
    a_pair = shifted(pair, 4)
    x_own = crossed(own, a_own)
    b_own = shifted(a_own, 4)
    state = attend((own, pair), qs, (own, pair), ((0, 0, 0), (1, 0, 0)), None)
    x_pair = crossed(pair, a_pair)
    b_pair = shifted(a_pair, 4)
    state = attend(
        (a_own, a_pair, x_own),
        qs,
        (a_own, a_pair, x_own),
        ((0, 4, 4), (1, 4, 4), (2, 4, 0)),
        state,
    )
    xb_own = crossed(a_own, b_own)
    xb_pair = crossed(a_pair, b_pair)
    state = attend(
        (b_own, b_pair, xb_own),
        qs,
        (x_pair, b_own, b_pair, xb_own),
        ((3, 4, 0), (0, 8, 8), (1, 8, 8), (2, 8, 4)),
        state,
    )
    full, out_send = attend((), qs, (xb_pair,), ((3, 8, 4),), state, width)
    return merge(exchanged(out_send, 1), full)


def solution(mesh):
    spec = P(("groups", "ctx"), None)
    return jax.shard_map(steps, mesh=mesh, in_specs=(spec,) * 4, out_specs=spec, check_vma=False)
```

profile of v0, /device:TPU:27, one launch (start us, length us, event | category | flops | bytes accessed | tf_op | source)
XLA Modules:
  0.0 60.1 jit_solution(16971598897540199137)
XLA Ops:
  0.0 1.2 %collective-permute-start.1 = (s32[1,2]{1,0:T(1,128)}, s32[1,2]{1,0:T(1,128)S(1)}, u32[]{:S(2)}, u32[]{:S(2)}) collective-permute-start(s32[1,2]{1,0:T(1,128)} %refs_0_.3), channel_id=1, source_target_pairs={{0,2},{1,3},{2,0},{3,1},{4,6},{5,7},{6,4},{7,5},{8,10},{9,11},{10,... | collective-permute-start | bytes 32 | tf_op jit(solution)/shard_map/ppermute | solution.py:30
  1.2 1.3 %collective-permute-done.1.refs_1_ = s32[1,2]{1,0:T(1,128)S(1)} collective-permute-done((s32[1,2]{1,0:T(1,128)}, s32[1,2]{1,0:T(1,128)S(1)}, u32[]{:S(2)}, u32[]{:S(2)}) %collective-permute-start.1) | collective-permute-done | bytes 40 | tf_op jit(solution)/shard_map/ppermute | solution.py:30
  2.6 0.9 %copy-done.3 = bf16[256,512]{1,0:T(8,128)(2,1)S(1)} copy-done((bf16[256,512]{1,0:T(8,128)(2,1)S(1)}, bf16[256,512]{1,0:T(8,128)(2,1)}, u32[]{:S(2)}) %copy-start.3) | copy-done | bytes 262168
  3.5 0.9 %copy-done.4 = bf16[256,512]{1,0:T(8,128)(2,1)S(1)} copy-done((bf16[256,512]{1,0:T(8,128)(2,1)S(1)}, bf16[256,512]{1,0:T(8,128)(2,1)}, u32[]{:S(2)}) %copy-start.4) | copy-done | bytes 262168
  5.8 1.9 %collective-permute-start.2 = (bf16[528,256]{1,0:T(8,128)(2,1)S(1)}, bf16[528,256]{1,0:T(8,128)(2,1)S(1)}, u32[]{:S(2)}, u32[]{:S(2)}) collective-permute-start(bf16[528,256]{1,0:T(8,128)(2,1)S(1)} %prep_kv.2), channel_id=1, source_target_pairs={{0,1},{1,0},{2,3},{3,2},{4,5},{5,4},{6,7},{7,6},{8,9},{9,8},{10,11... | collective-permute-start | bytes 811016 | tf_op jit(solution)/shard_map/ppermute | solution.py:30
  7.7 2.5 %prep_kv.3.lower_ref.refs_0_.refs_4_ = bf16[528,256]{1,0:T(8,128)(2,1)} custom-call(bf16[256,512]{1,0:T(8,128)(2,1)} %k_ref.3, bf16[256,512]{1,0:T(8,128)(2,1)} %v_ref.3, s32[1,2]{1,0:T(1,128)} %refs_0_.3), custom_call_target="tpu_custom_call" | custom-call | tf_op jit(solution)/shard_map/prep_kv/pallas_call | solution.py:72
  10.9 1.3 %collective-permute-start.3 = (bf16[528,256]{1,0:T(8,128)(2,1)S(1)}, bf16[528,256]{1,0:T(8,128)(2,1)S(1)}, u32[]{:S(2)}, u32[]{:S(2)}) collective-permute-start(bf16[528,256]{1,0:T(8,128)(2,1)S(1)} %collective-permute-done.2.lower_ref.refs_1_.refs_5_), channel_id=1, source_target_pairs={{0,4},{1,5},{2,6},{3,7},{4,8},{5,9},{6,10},{7,11},{8,12},{9,13},{1... | collective-permute-start | bytes 811016 | tf_op jit(solution)/shard_map/ppermute | solution.py:35
  12.2 6.3 %collective-permute-done.6.lower_ref.upper_ref.refs_0_.refs_5_ = bf16[528,256]{1,0:T(8,128)(2,1)S(1)} collective-permute-done((bf16[528,256]{1,0:T(8,128)(2,1)}, bf16[528,256]{1,0:T(8,128)(2,1)S(1)}, u32[]{:S(2)}, u32[]{:S(2)}) %collective-permute-start.6) | collective-permute-done | bytes 270368 | tf_op jit(solution)/shard_map/ppermute | solution.py:35
  18.5 1.9 %collective-permute-start.7 = (bf16[528,256]{1,0:T(8,128)(2,1)S(1)}, bf16[528,256]{1,0:T(8,128)(2,1)S(1)}, u32[]{:S(2)}, u32[]{:S(2)}) collective-permute-start(bf16[528,256]{1,0:T(8,128)(2,1)S(1)} %collective-permute-done.6.lower_ref.upper_ref.refs_0_.refs_5_), channel_id=1, source_target_pairs={{0,4},{1,5},{2,6},{3,7},{4,8},{5,9},{6,10},{7,11},{8,12},{9,13},{1... | collective-permute-start | bytes 811016 | tf_op jit(solution)/shard_map/ppermute | solution.py:35
  20.3 3.9 %collective-permute-done.3.lower_ref.upper_ref.refs_1_.refs_6_ = bf16[528,256]{1,0:T(8,128)(2,1)S(1)} collective-permute-done((bf16[528,256]{1,0:T(8,128)(2,1)S(1)}, bf16[528,256]{1,0:T(8,128)(2,1)S(1)}, u32[]{:S(2)}, u32[]{:S(2)}) %collective-permute-start.3) | collective-permute-done | bytes 270368 | tf_op jit(solution)/shard_map/ppermute | solution.py:35
  24.3 1.9 %collective-permute-start.4 = (bf16[528,256]{1,0:T(8,128)(2,1)S(1)}, bf16[528,256]{1,0:T(8,128)(2,1)S(1)}, u32[]{:S(2)}, u32[]{:S(2)}) collective-permute-start(bf16[528,256]{1,0:T(8,128)(2,1)S(1)} %collective-permute-done.3.lower_ref.upper_ref.refs_1_.refs_6_), channel_id=1, source_target_pairs={{0,4},{1,5},{2,6},{3,7},{4,8},{5,9},{6,10},{7,11},{8,12},{9,13},{1... | collective-permute-start | bytes 811016 | tf_op jit(solution)/shard_map/ppermute | solution.py:35
  26.1 1.0 %copy-done.1 = bf16[528,256]{1,0:T(8,128)(2,1)S(1)} copy-done((bf16[528,256]{1,0:T(8,128)(2,1)S(1)}, bf16[528,256]{1,0:T(8,128)(2,1)}, u32[]{:S(2)}) %copy-start.1) | copy-done | bytes 270360
  27.1 1.3 %collective-permute-start.10 = (bf16[528,256]{1,0:T(8,128)(2,1)S(1)}, bf16[528,256]{1,0:T(8,128)(2,1)S(1)}, u32[]{:S(2)}, u32[]{:S(2)}) collective-permute-start(bf16[528,256]{1,0:T(8,128)(2,1)S(1)} %pick.7), channel_id=1, source_target_pairs={{0,2},{1,3},{2,0},{3,1},{4,6},{5,7},{6,4},{7,5},{8,10},{9,11},{10,... | collective-permute-start | bytes 811016 | tf_op jit(solution)/shard_map/ppermute | solution.py:30
  28.4 1.6 %collective-permute-done.7.upper_ref.refs_0_.refs_6_ = bf16[528,256]{1,0:T(8,128)(2,1)S(1)} collective-permute-done((bf16[528,256]{1,0:T(8,128)(2,1)S(1)}, bf16[528,256]{1,0:T(8,128)(2,1)S(1)}, u32[]{:S(2)}, u32[]{:S(2)}) %collective-permute-start.7) | collective-permute-done | bytes 270368 | tf_op jit(solution)/shard_map/ppermute | solution.py:35
  30.1 1.3 %collective-permute-start.8 = (bf16[528,256]{1,0:T(8,128)(2,1)S(1)}, bf16[528,256]{1,0:T(8,128)(2,1)S(1)}, u32[]{:S(2)}, u32[]{:S(2)}) collective-permute-start(bf16[528,256]{1,0:T(8,128)(2,1)S(1)} %pick.5), channel_id=1, source_target_pairs={{0,2},{1,3},{2,0},{3,1},{4,6},{5,7},{6,4},{7,5},{8,10},{9,11},{10,... | collective-permute-start | bytes 811016 | tf_op jit(solution)/shard_map/ppermute | solution.py:30
  32.1 3.6 %attend.4 = (f32[2,2,128,1024]{3,2,1,0:T(8,128)S(1)}, f32[2,2,2,1,1024]{4,3,2,1,0:T(1,128)S(1)}, f32[4,1,128]{2,1,0:T(1,128)S(1)}) custom-call(bf16[528,256]{1,0:T(8,128)(2,1)S(1)} %copy-done.2, bf16[528,256]{1,0:T(8,128)(2,1)S(1)} %collective-permute-done.2.lower_ref.refs_1_.refs_5_, bf16[2,128,1024]{2,1,0:T(8,128)(2,1)S(1)} %prep_q.2.refs_2_.refs_3_.refs_0_, ...), custom_call_target="tpu_custom_call" | custom-call | flops 1073741824 | bytes 6291456 | tf_op jit(solution)/shard_map/attend/pallas_call | solution.py:358
  35.9 2.6 %collective-permute-start.5 = (bf16[528,256]{1,0:T(8,128)(2,1)S(1)}, bf16[528,256]{1,0:T(8,128)(2,1)S(1)}, u32[]{:S(2)}, u32[]{:S(2)}) collective-permute-start(bf16[528,256]{1,0:T(8,128)(2,1)S(1)} %pick.4), channel_id=1, source_target_pairs={{0,2},{1,3},{2,0},{3,1},{4,6},{5,7},{6,4},{7,5},{8,10},{9,11},{10,... | collective-permute-start | bytes 811016 | tf_op jit(solution)/shard_map/ppermute | solution.py:30
  38.5 4.8 %attend.5 = (f32[2,2,128,1024]{3,2,1,0:T(8,128)S(1)}, f32[2,2,2,1,1024]{4,3,2,1,0:T(1,128)S(1)}, f32[4,1,128]{2,1,0:T(1,128)S(1)}) custom-call(bf16[528,256]{1,0:T(8,128)(2,1)S(1)} %collective-permute-done.6.lower_ref.upper_ref.refs_0_.refs_5_, ...), custom_call_target="tpu_custom_call", output_to_operand_aliasing={{0}: (8, {}), {1}: (9, {}), {2}: (10, {})} | custom-call | flops 1610612736 | bytes 6291456 | tf_op jit(solution)/shard_map/attend/pallas_call | solution.py:358
  43.3 2.0 %collective-permute-done.9.refs_5_ = bf16[528,256]{1,0:T(8,128)(2,1)S(1)} collective-permute-done((bf16[528,256]{1,0:T(8,128)(2,1)S(1)}, bf16[528,256]{1,0:T(8,128)(2,1)S(1)}, u32[]{:S(2)}, u32[]{:S(2)}) %collective-permute-start.9) | collective-permute-done | bytes 270368 | tf_op jit(solution)/shard_map/ppermute | solution.py:30
  45.3 5.0 %attend.6 = (f32[2,2,128,1024]{3,2,1,0:T(8,128)S(1)}, f32[2,2,2,1,1024]{4,3,2,1,0:T(1,128)S(1)}, f32[4,1,128]{2,1,0:T(1,128)S(1)}) custom-call(bf16[528,256]{1,0:T(8,128)(2,1)S(1)} %collective-permute-done.7.upper_ref.refs_0_.refs_6_, ...), custom_call_target="tpu_custom_call", output_to_operand_aliasing={{0}: (9, {}), {1}: (10, {}), {2}: (11, {})} | custom-call | flops 2147483648 | bytes 6291456 | tf_op jit(solution)/shard_map/attend/pallas_call | solution.py:358
  51.1 3.1 %attend.7 = (bf16[256,2048]{1,0:T(8,128)(2,1)}, bf16[256,1024]{1,0:T(8,128)(2,1)S(1)}) custom-call(bf16[2,128,1024]{2,1,0:T(8,128)(2,1)S(1)} %prep_q.2.refs_2_.refs_3_.refs_0_, bf16[2,128,1024]{2,1,0:T(8,128)(2,1)S(1)} %collective-permute-done.refs_3_.refs_4_.refs_1_, bf16[528,256]{1,0:T(8,128)(2,1)S(1)} %collective-permute-done.5.refs_2_, ...), custom_call_target="tpu_custom_call" | custom-call | flops 536870912 | bytes 6291456 | tf_op jit(solution)/shard_map/attend/pallas_call | solution.py:358
  54.2 3.6 %collective-permute-start.11 = (bf16[256,1024]{1,0:T(8,128)(2,1)S(1)}, bf16[256,1024]{1,0:T(8,128)(2,1)S(1)}, u32[]{:S(2)}, u32[]{:S(2)}) collective-permute-start(bf16[256,1024]{1,0:T(8,128)(2,1)S(1)} %get-tuple-element.25), channel_id=1, source_target_pairs={{0,1},{1,0},{2,3},{3,2},{4,5},{5,4},{6,7},{7,6},{8,9},{9,8},{10,11... | collective-permute-start | bytes 1572872 | tf_op jit(solution)/shard_map/ppermute | solution.py:30
  57.8 1.5 %collective-permute-done.11.got_ref = bf16[256,1024]{1,0:T(8,128)(2,1)S(1)} collective-permute-done((bf16[256,1024]{1,0:T(8,128)(2,1)S(1)}, bf16[256,1024]{1,0:T(8,128)(2,1)S(1)}, u32[]{:S(2)}, u32[]{:S(2)}) %collective-permute-start.11) | collective-permute-done | bytes 524320 | tf_op jit(solution)/shard_map/ppermute | solution.py:30
  59.3 0.8 %merge.1 = bf16[256,2048]{1,0:T(8,128)(2,1)} custom-call(bf16[256,1024]{1,0:T(8,128)(2,1)S(1)} %collective-permute-done.11.got_ref, bf16[256,2048]{1,0:T(8,128)(2,1)} %get-tuple-element.26.full_in), custom_call_target="tpu_custom_call", output_to_operand_aliasing={{}: (1, {})} | custom-call | tf_op jit(solution)/shard_map/merge/pallas_call | solution.py:152
  (25 shorter events, 3.7 us)
Async XLA Ops:
  0.0 10.2 %copy-start = (bf16[256,2048]{1,0:T(8,128)(2,1)S(1)}, bf16[256,2048]{1,0:T(8,128)(2,1)}, u32[]{:S(2)}) copy-start(bf16[256,2048]{1,0:T(8,128)(2,1)} %q_ref.3) | copy-start | bytes 3145732
  0.0 2.6 %collective-permute-start.1 = (s32[1,2]{1,0:T(1,128)}, s32[1,2]{1,0:T(1,128)S(1)}, u32[]{:S(2)}, u32[]{:S(2)}) collective-permute-start(s32[1,2]{1,0:T(1,128)} %refs_0_.3), channel_id=1, source_target_pairs={{0,2},{1,3},{2,0},{3,1},{4,6},{5,7},{6,4},{7,5},{8,10},{9,11},{10,... | collective-permute-start | bytes 32 | tf_op jit(solution)/shard_map/ppermute | solution.py:30
  2.6 1.0 %copy-start.3 = (bf16[256,512]{1,0:T(8,128)(2,1)S(1)}, bf16[256,512]{1,0:T(8,128)(2,1)}, u32[]{:S(2)}) copy-start(bf16[256,512]{1,0:T(8,128)(2,1)} %k_ref.3) | copy-start | bytes 786436
  3.5 0.9 %copy-start.4 = (bf16[256,512]{1,0:T(8,128)(2,1)S(1)}, bf16[256,512]{1,0:T(8,128)(2,1)}, u32[]{:S(2)}) copy-start(bf16[256,512]{1,0:T(8,128)(2,1)} %v_ref.3) | copy-start | bytes 786436
  4.5 0.7 %copy-start.5 = (s32[1,2]{1,0:T(1,128)S(1)}, s32[1,2]{1,0:T(1,128)}, u32[]{:S(2)}) copy-start(s32[1,2]{1,0:T(1,128)} %refs_0_.3) | copy-start | bytes 28
  5.8 5.0 %collective-permute-start.2 = (bf16[528,256]{1,0:T(8,128)(2,1)S(1)}, bf16[528,256]{1,0:T(8,128)(2,1)S(1)}, u32[]{:S(2)}, u32[]{:S(2)}) collective-permute-start(bf16[528,256]{1,0:T(8,128)(2,1)S(1)} %prep_kv.2), channel_id=1, source_target_pairs={{0,1},{1,0},{2,3},{3,2},{4,5},{5,4},{6,7},{7,6},{8,9},{9,8},{10,11... | collective-permute-start | bytes 811016 | tf_op jit(solution)/shard_map/ppermute | solution.py:30
  10.2 8.3 %collective-permute-start.6 = (bf16[528,256]{1,0:T(8,128)(2,1)}, bf16[528,256]{1,0:T(8,128)(2,1)S(1)}, u32[]{:S(2)}, u32[]{:S(2)}) collective-permute-start(bf16[528,256]{1,0:T(8,128)(2,1)} %prep_kv.3.lower_ref.refs_0_.refs_4_), channel_id=1, source_target_pairs={{0,4},{1,5},{2,6},{3,7},{4,8},{5,9},{6,10},{7,11},{8,12},{9,13},{1... | collective-permute-start | bytes 811016 | tf_op jit(solution)/shard_map/ppermute | solution.py:35
  10.3 21.8 %copy-start.2 = (bf16[528,256]{1,0:T(8,128)(2,1)S(1)}, bf16[528,256]{1,0:T(8,128)(2,1)}, u32[]{:S(2)}) copy-start(bf16[528,256]{1,0:T(8,128)(2,1)} %prep_kv.3.lower_ref.refs_0_.refs_4_) | copy-start | bytes 811012
  10.6 21.5 %collective-permute-start = (bf16[2,128,1024]{2,1,0:T(8,128)(2,1)S(1)}, bf16[2,128,1024]{2,1,0:T(8,128)(2,1)S(1)}, u32[]{:S(2)}, u32[]{:S(2)}) collective-permute-start(bf16[2,128,1024]{2,1,0:T(8,128)(2,1)S(1)} %prep_q.3), channel_id=1, source_target_pairs={{0,1},{1,0},{2,3},{3,2},{4,5},{5,4},{6,7},{7,6},{8,9},{9,8},{10,11... | collective-permute-start | bytes 1572872 | tf_op jit(solution)/shard_map/ppermute | solution.py:30
  10.9 13.4 %collective-permute-start.3 = (bf16[528,256]{1,0:T(8,128)(2,1)S(1)}, bf16[528,256]{1,0:T(8,128)(2,1)S(1)}, u32[]{:S(2)}, u32[]{:S(2)}) collective-permute-start(bf16[528,256]{1,0:T(8,128)(2,1)S(1)} %collective-permute-done.2.lower_ref.refs_1_.refs_5_), channel_id=1, source_target_pairs={{0,4},{1,5},{2,6},{3,7},{4,8},{5,9},{6,10},{7,11},{8,12},{9,13},{1... | collective-permute-start | bytes 811016 | tf_op jit(solution)/shard_map/ppermute | solution.py:35
  18.5 11.6 %collective-permute-start.7 = (bf16[528,256]{1,0:T(8,128)(2,1)S(1)}, bf16[528,256]{1,0:T(8,128)(2,1)S(1)}, u32[]{:S(2)}, u32[]{:S(2)}) collective-permute-start(bf16[528,256]{1,0:T(8,128)(2,1)S(1)} %collective-permute-done.6.lower_ref.upper_ref.refs_0_.refs_5_), channel_id=1, source_target_pairs={{0,4},{1,5},{2,6},{3,7},{4,8},{5,9},{6,10},{7,11},{8,12},{9,13},{1... | collective-permute-start | bytes 811016 | tf_op jit(solution)/shard_map/ppermute | solution.py:35
  24.3 11.6 %collective-permute-start.4 = (bf16[528,256]{1,0:T(8,128)(2,1)S(1)}, bf16[528,256]{1,0:T(8,128)(2,1)S(1)}, u32[]{:S(2)}, u32[]{:S(2)}) collective-permute-start(bf16[528,256]{1,0:T(8,128)(2,1)S(1)} %collective-permute-done.3.lower_ref.upper_ref.refs_1_.refs_6_), channel_id=1, source_target_pairs={{0,4},{1,5},{2,6},{3,7},{4,8},{5,9},{6,10},{7,11},{8,12},{9,13},{1... | collective-permute-start | bytes 811016 | tf_op jit(solution)/shard_map/ppermute | solution.py:35
  26.1 1.0 %copy-start.1 = (bf16[528,256]{1,0:T(8,128)(2,1)S(1)}, bf16[528,256]{1,0:T(8,128)(2,1)}, u32[]{:S(2)}) copy-start(bf16[528,256]{1,0:T(8,128)(2,1)} %prep_kv.3.lower_ref.refs_0_.refs_4_) | copy-start | bytes 811012
  27.1 11.4 %collective-permute-start.10 = (bf16[528,256]{1,0:T(8,128)(2,1)S(1)}, bf16[528,256]{1,0:T(8,128)(2,1)S(1)}, u32[]{:S(2)}, u32[]{:S(2)}) collective-permute-start(bf16[528,256]{1,0:T(8,128)(2,1)S(1)} %pick.7), channel_id=1, source_target_pairs={{0,2},{1,3},{2,0},{3,1},{4,6},{5,7},{6,4},{7,5},{8,10},{9,11},{10,... | collective-permute-start | bytes 811016 | tf_op jit(solution)/shard_map/ppermute | solution.py:30
  30.1 13.2 %collective-permute-start.8 = (bf16[528,256]{1,0:T(8,128)(2,1)S(1)}, bf16[528,256]{1,0:T(8,128)(2,1)S(1)}, u32[]{:S(2)}, u32[]{:S(2)}) collective-permute-start(bf16[528,256]{1,0:T(8,128)(2,1)S(1)} %pick.5), channel_id=1, source_target_pairs={{0,2},{1,3},{2,0},{3,1},{4,6},{5,7},{6,4},{7,5},{8,10},{9,11},{10,... | collective-permute-start | bytes 811016 | tf_op jit(solution)/shard_map/ppermute | solution.py:30
  31.4 13.9 %collective-permute-start.9 = (bf16[528,256]{1,0:T(8,128)(2,1)S(1)}, bf16[528,256]{1,0:T(8,128)(2,1)S(1)}, u32[]{:S(2)}, u32[]{:S(2)}) collective-permute-start(bf16[528,256]{1,0:T(8,128)(2,1)S(1)} %pick.6), channel_id=1, source_target_pairs={{0,2},{1,3},{2,0},{3,1},{4,6},{5,7},{6,4},{7,5},{8,10},{9,11},{10,... | collective-permute-start | bytes 811016 | tf_op jit(solution)/shard_map/ppermute | solution.py:30
  35.9 15.2 %collective-permute-start.5 = (bf16[528,256]{1,0:T(8,128)(2,1)S(1)}, bf16[528,256]{1,0:T(8,128)(2,1)S(1)}, u32[]{:S(2)}, u32[]{:S(2)}) collective-permute-start(bf16[528,256]{1,0:T(8,128)(2,1)S(1)} %pick.4), channel_id=1, source_target_pairs={{0,2},{1,3},{2,0},{3,1},{4,6},{5,7},{6,4},{7,5},{8,10},{9,11},{10,... | collective-permute-start | bytes 811016 | tf_op jit(solution)/shard_map/ppermute | solution.py:30
  54.2 5.2 %collective-permute-start.11 = (bf16[256,1024]{1,0:T(8,128)(2,1)S(1)}, bf16[256,1024]{1,0:T(8,128)(2,1)S(1)}, u32[]{:S(2)}, u32[]{:S(2)}) collective-permute-start(bf16[256,1024]{1,0:T(8,128)(2,1)S(1)} %get-tuple-element.25), channel_id=1, source_target_pairs={{0,1},{1,0},{2,3},{3,2},{4,5},{5,4},{6,7},{7,6},{8,9},{9,8},{10,11... | collective-permute-start | bytes 1572872 | tf_op jit(solution)/shard_map/ppermute | solution.py:30
where the time goes:
time: 60.4 us; the launch traced here: 60.1 us
  Pallas kernels  21.2 us (35%)
  waiting for transfers between devices  17.7 us (29%)
  starting transfers between devices  17.6 us (29%)
  local copies, waits for them, and re-layouts  3.51 us (6%)
    pallas_call x4, Pallas kernels, attend(): pl.pallas_call(functools.partial(attend_kernel, sources, len(infos), firs...  16.5 us
    ppermute x8, starting transfers between devices, exchanged(): return lax.ppermute(x, 'ctx', [(i, i ^ bit) for i in range(n)])  12.5 us
    ppermute x4, waiting for transfers between devices, shifted(): return lax.ppermute(x, 'ctx', [(i, (i + distance) % n) for i in range(n)])  12 us
    ppermute x8, waiting for transfers between devices, exchanged(): return lax.ppermute(x, 'ctx', [(i, i ^ bit) for i in range(n)])  5.67 us
    ppermute x4, starting transfers between devices, shifted(): return lax.ppermute(x, 'ctx', [(i, (i + distance) % n) for i in range(n)])  5.08 us
    unnamed x12, local copies, waits for them, and re-layouts  3.51 us
    pallas_call x2, Pallas kernels, prep_kv(): pl.pallas_call(functools.partial(prep_kv_kernel, other), out_shape=jax.Sh...  3.16 us
  transfers between devices with their start and end apart: 12, of which 8 were waited for; matrix products, arithmetic and copies ran while one was open for 0% of the time, Pallas kernels for 28%

commit v1 on v0

--- a/solution.py
+++ b/solution.py
@@ -44,38 +44,68 @@
     return pl.ds(pl.multiple_of(index * width, width), width)
 
 
-def prep_kv_kernel(other, k_ref, v_ref, *refs):
-    *tables, out_ref, k_buf, v_buf, sems = refs
+def prep_kv_kernel(other, count, k_ref, v_ref, *refs):
+    table_refs, (out_ref, k_buf, v_buf, turned, info_buf) = refs[:count], refs[count : count + 5]
+    tables, sems, out_sems = refs[count + 5 :]
     pick = my_half(other)
-    copies = [
-        pltpu.make_async_copy(ref.at[:, columns(pick, 2 * HD)], buf, sems.at[i])
-        for i, (ref, buf) in enumerate(((k_ref, k_buf), (v_ref, v_buf)))
-    ]
-    for copy in copies:
+    rows = LEN // 2
+    fetch = pltpu.make_async_copy
+    starts = [fetch(ref, tables.at[i], sems.at[4 + i]) for i, ref in enumerate(table_refs)]
+    v_in = [
+        fetch(v_ref.at[i * rows : (i + 1) * rows, columns(pick, 2 * HD)], v_buf.at[i], sems.at[i])
+        for i in range(2)
+    ]
+    k_in = [
+        fetch(k_ref.at[i * rows : (i + 1) * rows, columns(pick, 2 * HD)], k_buf.at[i], sems.at[2 + i])
+        for i in range(2)
+    ]
+    for copy in starts + v_in + k_in:
         copy.start()
+    leaving = []
+
+    def leave(source, first, last):
+        copy = fetch(source, out_ref.at[first:last], out_sems.at[len(leaving)])
+        copy.start()
+        leaving.append(copy)
+
+    for copy in starts:
+        copy.wait()
     lane = lax.broadcasted_iota(jnp.int32, (16, LEN), 1)
     info = jnp.full((16, LEN), -1, jnp.int32)
-    slot = 0
-    for table in tables:
+    for i in range(count):
         for col in range(2):
-            info = jnp.where(lane == slot, table[0, col], info)
-            slot += 1
-    out_ref[INFO:, :] = info.astype(jnp.float32).astype(jnp.bfloat16)
-    copies[1].wait()
-    for pair in range(2):
-        out_ref[LEN + pair * HD : LEN + (pair + 1) * HD, :] = v_buf[:, pair * HD : (pair + 1) * HD].T
-    copies[0].wait()
-    out_ref[:LEN, :] = k_buf[...]
+            info = jnp.where(lane == 2 * i + col, tables[i, 0, col], info)
+    info_buf[...] = info.astype(jnp.float32).astype(jnp.bfloat16)
+    leave(info_buf, INFO, INFO + 16)
+    for i, copy in enumerate(v_in):
+        copy.wait()
+        for pair in range(2):
+            turned[pair * HD : (pair + 1) * HD, i * rows : (i + 1) * rows] = v_buf[
+                i, :, pair * HD : (pair + 1) * HD
+            ].T
+    leave(turned, LEN, INFO)
+    for i, copy in enumerate(k_in):
+        copy.wait()
+        leave(k_buf.at[i], i * rows, (i + 1) * rows)
+    for copy in leaving:
+        copy.wait()
 
 
 def prep_kv(keys, values, tables, other):
     return pl.pallas_call(
-        functools.partial(prep_kv_kernel, other),
+        functools.partial(prep_kv_kernel, other, len(tables)),
         out_shape=jax.ShapeDtypeStruct(CHUNK, jnp.bfloat16),
-        in_specs=[ANY, ANY] + [SMEM] * len(tables),
-        out_specs=VMEM,
-        scratch_shapes=[pltpu.VMEM((LEN, LEN), jnp.bfloat16)] * 2 + [pltpu.SemaphoreType.DMA((2,))],
-        compiler_params=pltpu.CompilerParams(vmem_limit_bytes=4 << 20 if other else None),
+        in_specs=[ANY] * (2 + len(tables)),
+        out_specs=ANY,
+        scratch_shapes=[
+            pltpu.VMEM((2, LEN // 2, LEN), jnp.bfloat16),
+            pltpu.VMEM((2, LEN // 2, LEN), jnp.bfloat16),
+            pltpu.VMEM((LEN, LEN), jnp.bfloat16),
+            pltpu.VMEM((16, LEN), jnp.bfloat16),
+            pltpu.SMEM((len(tables), 1, 2), jnp.int32),
+            pltpu.SemaphoreType.DMA((4 + len(tables),)),
+            pltpu.SemaphoreType.DMA((4,)),
+        ],
         name="prep_kv",
     )(keys, values, *tables)
 
@@ -387,20 +417,16 @@
     state = attend((own, pair), qs, (own, pair), ((0, 0, 0), (1, 0, 0)), None)
     x_pair = crossed(pair, a_pair)
     b_pair = shifted(a_pair, 4)
-    state = attend(
-        (a_own, a_pair, x_own),
-        qs,
-        (a_own, a_pair, x_own),
-        ((0, 4, 4), (1, 4, 4), (2, 4, 0)),
-        state,
-    )
+    state = attend((a_own, a_pair, x_own), qs, (a_own,), ((0, 4, 4),), state)
     xb_own = crossed(a_own, b_own)
+    state = attend((), qs, (a_pair, x_own), ((1, 4, 4), (2, 4, 0)), state)
     xb_pair = crossed(a_pair, b_pair)
+    state = attend((), qs, (x_pair,), ((3, 4, 0),), state)
     state = attend(
         (b_own, b_pair, xb_own),
         qs,
-        (x_pair, b_own, b_pair, xb_own),
-        ((3, 4, 0), (0, 8, 8), (1, 8, 8), (2, 8, 4)),
+        (b_own, b_pair, xb_own),
+        ((0, 8, 8), (1, 8, 8), (2, 8, 4)),
         state,
     )
     full, out_send = attend((), qs, (xb_pair,), ((3, 8, 4),), state, width)

time: 60.4 us -> 56.3 us (0.932)
  the two profiles are of different devices: /device:TPU:27 before, /device:TPU:23 now
where the time goes in v1:
time: 56.3 us; the launch traced here: 56.1 us
  Pallas kernels  28 us (50%)
  waiting for transfers between devices  17.5 us (31%)
  starting transfers between devices  8.92 us (16%)
  local copies, waits for them, and re-layouts  1.48 us (3%)
    pallas_call x6, Pallas kernels, attend(): pl.pallas_call(functools.partial(attend_kernel, sources, len(infos), firs...  22.9 us
    ppermute x4, waiting for transfers between devices, shifted(): return lax.ppermute(x, 'ctx', [(i, (i + distance) % n) for i in range(n)])  13.3 us
    ppermute x8, starting transfers between devices, exchanged(): return lax.ppermute(x, 'ctx', [(i, i ^ bit) for i in range(n)])  4.98 us
    ppermute x8, waiting for transfers between devices, exchanged(): return lax.ppermute(x, 'ctx', [(i, i ^ bit) for i in range(n)])  4.24 us
    ppermute x4, starting transfers between devices, shifted(): return lax.ppermute(x, 'ctx', [(i, (i + distance) % n) for i in range(n)])  3.94 us
    pallas_call x2, Pallas kernels, prep_kv(): pl.pallas_call(functools.partial(prep_kv_kernel, other, len(tables)), out...  3.52 us
    unnamed x8, local copies, waits for them, and re-layouts  1.48 us
  transfers between devices with their start and end apart: 12, of which 5 were waited for; matrix products, arithmetic and copies ran while one was open for 0% of the time, Pallas kernels for 42%

profile of v1, /device:TPU:23, one launch (start us, length us, event | category | flops | bytes accessed | tf_op | source)
XLA Modules:
  0.0 56.1 jit_solution(12368421859576905706)
XLA Ops:
  0.2 2.3 %collective-permute-done.1.refs_1_ = s32[1,2]{1,0:T(1,128)S(1)} collective-permute-done((s32[1,2]{1,0:T(1,128)}, s32[1,2]{1,0:T(1,128)S(1)}, u32[]{:S(2)}, u32[]{:S(2)}) %collective-permute-start.1) | collective-permute-done | bytes 40 | tf_op jit(solution)/shard_map/ppermute | solution.py:30
  2.6 0.5 copy-done.3
  3.1 1.8 %prep_kv.2 = bf16[528,256]{1,0:T(8,128)(2,1)} custom-call(bf16[256,512]{1,0:T(8,128)(2,1)} %k_ref.3, bf16[256,512]{1,0:T(8,128)(2,1)} %v_ref.3, s32[1,2]{1,0:T(1,128)} %refs_0_.3, s32[1,2]{1,0:T(1,128)} %copy-done.3), custom_call_target="tpu_custom_call" | custom-call | tf_op jit(solution)/shard_map/prep_kv/pallas_call | solution.py:95
  4.9 1.9 %collective-permute-start.2 = (bf16[528,256]{1,0:T(8,128)(2,1)}, bf16[528,256]{1,0:T(8,128)(2,1)S(1)}, u32[]{:S(2)}, u32[]{:S(2)}) collective-permute-start(bf16[528,256]{1,0:T(8,128)(2,1)} %prep_kv.2), channel_id=1, source_target_pairs={{0,1},{1,0},{2,3},{3,2},{4,5},{5,4},{6,7},{7,6},{8,9},{9,8},{10,11... | collective-permute-start | bytes 811016 | tf_op jit(solution)/shard_map/ppermute | solution.py:30
  6.7 1.8 %prep_kv.3.lower_ref.refs_0_.refs_4_ = bf16[528,256]{1,0:T(8,128)(2,1)} custom-call(bf16[256,512]{1,0:T(8,128)(2,1)} %k_ref.3, bf16[256,512]{1,0:T(8,128)(2,1)} %v_ref.3, s32[1,2]{1,0:T(1,128)} %refs_0_.3), custom_call_target="tpu_custom_call" | custom-call | tf_op jit(solution)/shard_map/prep_kv/pallas_call | solution.py:95
  8.5 1.3 %collective-permute-start.6 = (bf16[528,256]{1,0:T(8,128)(2,1)}, bf16[528,256]{1,0:T(8,128)(2,1)S(1)}, u32[]{:S(2)}, u32[]{:S(2)}) collective-permute-start(bf16[528,256]{1,0:T(8,128)(2,1)} %prep_kv.3.lower_ref.refs_0_.refs_4_), channel_id=1, source_target_pairs={{0,4},{1,5},{2,6},{3,7},{4,8},{5,9},{6,10},{7,11},{8,12},{9,13},{1... | collective-permute-start | bytes 811016 | tf_op jit(solution)/shard_map/ppermute | solution.py:35
  9.9 0.3 prep_q.3
  10.2 0.4 collective-permute-start
  10.6 6.2 %collective-permute-done.6.lower_ref.upper_ref.refs_0_.refs_5_ = bf16[528,256]{1,0:T(8,128)(2,1)S(1)} collective-permute-done((bf16[528,256]{1,0:T(8,128)(2,1)}, bf16[528,256]{1,0:T(8,128)(2,1)S(1)}, u32[]{:S(2)}, u32[]{:S(2)}) %collective-permute-start.6) | collective-permute-done | bytes 270368 | tf_op jit(solution)/shard_map/ppermute | solution.py:35
  16.8 1.3 %collective-permute-start.7 = (bf16[528,256]{1,0:T(8,128)(2,1)S(1)}, bf16[528,256]{1,0:T(8,128)(2,1)S(1)}, u32[]{:S(2)}, u32[]{:S(2)}) collective-permute-start(bf16[528,256]{1,0:T(8,128)(2,1)S(1)} %collective-permute-done.6.lower_ref.upper_ref.refs_0_.refs_5_), channel_id=1, source_target_pairs={{0,4},{1,5},{2,6},{3,7},{4,8},{5,9},{6,10},{7,11},{8,12},{9,13},{1... | collective-permute-start | bytes 811016 | tf_op jit(solution)/shard_map/ppermute | solution.py:35
  18.1 1.0 %copy-done.1 = bf16[528,256]{1,0:T(8,128)(2,1)S(1)} copy-done((bf16[528,256]{1,0:T(8,128)(2,1)S(1)}, bf16[528,256]{1,0:T(8,128)(2,1)}, u32[]{:S(2)}) %copy-start.1) | copy-done | bytes 270360
  19.4 3.2 %collective-permute-done.3.lower_ref.upper_ref.refs_1_.refs_2_ = bf16[528,256]{1,0:T(8,128)(2,1)S(1)} collective-permute-done((bf16[528,256]{1,0:T(8,128)(2,1)S(1)}, bf16[528,256]{1,0:T(8,128)(2,1)S(1)}, u32[]{:S(2)}, u32[]{:S(2)}) %collective-permute-start.3) | collective-permute-done | bytes 270368 | tf_op jit(solution)/shard_map/ppermute | solution.py:35
  22.6 1.3 %collective-permute-start.4 = (bf16[528,256]{1,0:T(8,128)(2,1)S(1)}, bf16[528,256]{1,0:T(8,128)(2,1)S(1)}, u32[]{:S(2)}, u32[]{:S(2)}) collective-permute-start(bf16[528,256]{1,0:T(8,128)(2,1)S(1)} %collective-permute-done.3.lower_ref.upper_ref.refs_1_.refs_2_), channel_id=1, source_target_pairs={{0,4},{1,5},{2,6},{3,7},{4,8},{5,9},{6,10},{7,11},{8,12},{9,13},{1... | collective-permute-start | bytes 811016 | tf_op jit(solution)/shard_map/ppermute | solution.py:35
  24.2 0.3 prep_q.2.refs_2_.refs_3_.refs_0_
  24.5 3.9 %collective-permute-done.7.upper_ref.refs_0_.refs_5_ = bf16[528,256]{1,0:T(8,128)(2,1)S(1)} collective-permute-done((bf16[528,256]{1,0:T(8,128)(2,1)S(1)}, bf16[528,256]{1,0:T(8,128)(2,1)S(1)}, u32[]{:S(2)}, u32[]{:S(2)}) %collective-permute-start.7) | collective-permute-done | bytes 270368 | tf_op jit(solution)/shard_map/ppermute | solution.py:35
  28.7 4.9 %attend.6 = (f32[2,2,128,1024]{3,2,1,0:T(8,128)S(1)}, f32[2,2,2,1,1024]{4,3,2,1,0:T(1,128)S(1)}, f32[4,1,128]{2,1,0:T(1,128)S(1)}) custom-call(bf16[528,256]{1,0:T(8,128)(2,1)S(1)} %copy-done.2, bf16[528,256]{1,0:T(8,128)(2,1)S(1)} %collective-permute-done.2.lower_ref.refs_1_.refs_5_, bf16[2,128,1024]{2,1,0:T(8,128)(2,1)S(1)} %prep_q.2.refs_2_.refs_3_.refs_0_, ...), custom_call_target="tpu_custom_call" | custom-call | flops 1073741824 | bytes 6291456 | tf_op jit(solution)/shard_map/attend/pallas_call | solution.py:388
  33.6 3.3 %attend.7 = (f32[2,2,128,1024]{3,2,1,0:T(8,128)S(1)}, f32[2,2,2,1,1024]{4,3,2,1,0:T(1,128)S(1)}, f32[4,1,128]{2,1,0:T(1,128)S(1)}) custom-call(bf16[528,256]{1,0:T(8,128)(2,1)S(1)} %collective-permute-done.6.lower_ref.upper_ref.refs_0_.refs_5_, ...), custom_call_target="tpu_custom_call", output_to_operand_aliasing={{0}: (6, {}), {1}: (7, {}), {2}: (8, {})} | custom-call | flops 536870912 | bytes 6291456 | tf_op jit(solution)/shard_map/attend/pallas_call | solution.py:388
  37.0 1.6 %collective-permute-start.5 = (bf16[528,256]{1,0:T(8,128)(2,1)S(1)}, bf16[528,256]{1,0:T(8,128)(2,1)S(1)}, u32[]{:S(2)}, u32[]{:S(2)}) collective-permute-start(bf16[528,256]{1,0:T(8,128)(2,1)S(1)} %pick.4), channel_id=1, source_target_pairs={{0,2},{1,3},{2,0},{3,1},{4,6},{5,7},{6,4},{7,5},{8,10},{9,11},{10,... | collective-permute-start | bytes 811016 | tf_op jit(solution)/shard_map/ppermute | solution.py:30
  38.6 5.9 %attend.8 = (f32[2,2,128,1024]{3,2,1,0:T(8,128)S(1)}, f32[2,2,2,1,1024]{4,3,2,1,0:T(1,128)S(1)}, f32[4,1,128]{2,1,0:T(1,128)S(1)}) custom-call(bf16[2,128,1024]{2,1,0:T(8,128)(2,1)S(1)} %prep_q.2.refs_2_.refs_3_.refs_0_, ...), custom_call_target="tpu_custom_call", output_to_operand_aliasing={{0}: (4, {}), {1}: (5, {}), {2}: (6, {})} | custom-call | flops 1073741824 | bytes 6291456 | tf_op jit(solution)/shard_map/attend/pallas_call | solution.py:388
  44.5 3.3 %attend.9 = (f32[2,2,128,1024]{3,2,1,0:T(8,128)S(1)}, f32[2,2,2,1,1024]{4,3,2,1,0:T(1,128)S(1)}, f32[4,1,128]{2,1,0:T(1,128)S(1)}) custom-call(bf16[2,128,1024]{2,1,0:T(8,128)(2,1)S(1)} %prep_q.2.refs_2_.refs_3_.refs_0_, ...), custom_call_target="tpu_custom_call", output_to_operand_aliasing={{0}: (3, {}), {1}: (4, {}), {2}: (5, {})} | custom-call | flops 536870912 | bytes 6291456 | tf_op jit(solution)/shard_map/attend/pallas_call | solution.py:388
  47.8 3.8 %attend.10 = (f32[2,2,128,1024]{3,2,1,0:T(8,128)S(1)}, f32[2,2,2,1,1024]{4,3,2,1,0:T(1,128)S(1)}, f32[4,1,128]{2,1,0:T(1,128)S(1)}) custom-call(bf16[528,256]{1,0:T(8,128)(2,1)S(1)} %collective-permute-done.7.upper_ref.refs_0_.refs_5_, ...), custom_call_target="tpu_custom_call", output_to_operand_aliasing={{0}: (8, {}), {1}: (9, {}), {2}: (10, {})} | custom-call | flops 1610612736 | bytes 6291456 | tf_op jit(solution)/shard_map/attend/pallas_call | solution.py:388
  51.6 1.8 %attend.11 = (bf16[256,2048]{1,0:T(8,128)(2,1)}, bf16[256,1024]{1,0:T(8,128)(2,1)S(1)}) custom-call(bf16[2,128,1024]{2,1,0:T(8,128)(2,1)S(1)} %prep_q.2.refs_2_.refs_3_.refs_0_, bf16[2,128,1024]{2,1,0:T(8,128)(2,1)S(1)} %collective-permute-done.refs_3_.refs_4_.refs_1_, bf16[528,256]{1,0:T(8,128)(2,1)S(1)} %collective-permute-done.5.refs_2_, ...), custom_call_target="tpu_custom_call" | custom-call | flops 536870912 | bytes 6291456 | tf_op jit(solution)/shard_map/attend/pallas_call | solution.py:388
  53.4 1.9 %collective-permute-done.11.got_ref = bf16[256,1024]{1,0:T(8,128)(2,1)S(1)} collective-permute-done((bf16[256,1024]{1,0:T(8,128)(2,1)S(1)}, bf16[256,1024]{1,0:T(8,128)(2,1)S(1)}, u32[]{:S(2)}, u32[]{:S(2)}) %collective-permute-start.11) | collective-permute-done | bytes 524320 | tf_op jit(solution)/shard_map/ppermute | solution.py:30
  55.3 0.8 %merge.1 = bf16[256,2048]{1,0:T(8,128)(2,1)} custom-call(bf16[256,1024]{1,0:T(8,128)(2,1)S(1)} %collective-permute-done.11.got_ref, bf16[256,2048]{1,0:T(8,128)(2,1)} %get-tuple-element.38.full_in), custom_call_target="tpu_custom_call", output_to_operand_aliasing={{}: (1, {})} | custom-call | tf_op jit(solution)/shard_map/merge/pallas_call | solution.py:182
  (23 shorter events, 1.4 us)
Async XLA Ops:
  0.0 9.9 %copy-start = (bf16[256,2048]{1,0:T(8,128)(2,1)S(1)}, bf16[256,2048]{1,0:T(8,128)(2,1)}, u32[]{:S(2)}) copy-start(bf16[256,2048]{1,0:T(8,128)(2,1)} %q_ref.3) | copy-start | bytes 3145732
  0.0 2.6 %collective-permute-start.1 = (s32[1,2]{1,0:T(1,128)}, s32[1,2]{1,0:T(1,128)S(1)}, u32[]{:S(2)}, u32[]{:S(2)}) collective-permute-start(s32[1,2]{1,0:T(1,128)} %refs_0_.3), channel_id=1, source_target_pairs={{0,2},{1,3},{2,0},{3,1},{4,6},{5,7},{6,4},{7,5},{8,10},{9,11},{10,... | collective-permute-start | bytes 32 | tf_op jit(solution)/shard_map/ppermute | solution.py:30
  2.6 0.5 copy-start.3
  4.9 5.7 %collective-permute-start.2 = (bf16[528,256]{1,0:T(8,128)(2,1)}, bf16[528,256]{1,0:T(8,128)(2,1)S(1)}, u32[]{:S(2)}, u32[]{:S(2)}) collective-permute-start(bf16[528,256]{1,0:T(8,128)(2,1)} %prep_kv.2), channel_id=1, source_target_pairs={{0,1},{1,0},{2,3},{3,2},{4,5},{5,4},{6,7},{7,6},{8,9},{9,8},{10,11... | collective-permute-start | bytes 811016 | tf_op jit(solution)/shard_map/ppermute | solution.py:30
  8.5 8.3 %collective-permute-start.6 = (bf16[528,256]{1,0:T(8,128)(2,1)}, bf16[528,256]{1,0:T(8,128)(2,1)S(1)}, u32[]{:S(2)}, u32[]{:S(2)}) collective-permute-start(bf16[528,256]{1,0:T(8,128)(2,1)} %prep_kv.3.lower_ref.refs_0_.refs_4_), channel_id=1, source_target_pairs={{0,4},{1,5},{2,6},{3,7},{4,8},{5,9},{6,10},{7,11},{8,12},{9,13},{1... | collective-permute-start | bytes 811016 | tf_op jit(solution)/shard_map/ppermute | solution.py:35
  9.9 18.9 %copy-start.2 = (bf16[528,256]{1,0:T(8,128)(2,1)S(1)}, bf16[528,256]{1,0:T(8,128)(2,1)}, u32[]{:S(2)}) copy-start(bf16[528,256]{1,0:T(8,128)(2,1)} %prep_kv.3.lower_ref.refs_0_.refs_4_) | copy-start | bytes 811012
  10.2 18.5 %collective-permute-start = (bf16[2,128,1024]{2,1,0:T(8,128)(2,1)S(1)}, bf16[2,128,1024]{2,1,0:T(8,128)(2,1)S(1)}, u32[]{:S(2)}, u32[]{:S(2)}) collective-permute-start(bf16[2,128,1024]{2,1,0:T(8,128)(2,1)S(1)} %prep_q.3), channel_id=1, source_target_pairs={{0,1},{1,0},{2,3},{3,2},{4,5},{5,4},{6,7},{7,6},{8,9},{9,8},{10,11... | collective-permute-start | bytes 1572872 | tf_op jit(solution)/shard_map/ppermute | solution.py:30
  10.5 12.0 %collective-permute-start.3 = (bf16[528,256]{1,0:T(8,128)(2,1)S(1)}, bf16[528,256]{1,0:T(8,128)(2,1)S(1)}, u32[]{:S(2)}, u32[]{:S(2)}) collective-permute-start(bf16[528,256]{1,0:T(8,128)(2,1)S(1)} %collective-permute-done.2.lower_ref.refs_1_.refs_5_), channel_id=1, source_target_pairs={{0,4},{1,5},{2,6},{3,7},{4,8},{5,9},{6,10},{7,11},{8,12},{9,13},{1... | collective-permute-start | bytes 811016 | tf_op jit(solution)/shard_map/ppermute | solution.py:35
  16.8 11.6 %collective-permute-start.7 = (bf16[528,256]{1,0:T(8,128)(2,1)S(1)}, bf16[528,256]{1,0:T(8,128)(2,1)S(1)}, u32[]{:S(2)}, u32[]{:S(2)}) collective-permute-start(bf16[528,256]{1,0:T(8,128)(2,1)S(1)} %collective-permute-done.6.lower_ref.upper_ref.refs_0_.refs_5_), channel_id=1, source_target_pairs={{0,4},{1,5},{2,6},{3,7},{4,8},{5,9},{6,10},{7,11},{8,12},{9,13},{1... | collective-permute-start | bytes 811016 | tf_op jit(solution)/shard_map/ppermute | solution.py:35
  18.1 1.0 %copy-start.1 = (bf16[528,256]{1,0:T(8,128)(2,1)S(1)}, bf16[528,256]{1,0:T(8,128)(2,1)}, u32[]{:S(2)}) copy-start(bf16[528,256]{1,0:T(8,128)(2,1)} %prep_kv.3.lower_ref.refs_0_.refs_4_) | copy-start | bytes 811012
  19.1 14.5 %collective-permute-start.10 = (bf16[528,256]{1,0:T(8,128)(2,1)S(1)}, bf16[528,256]{1,0:T(8,128)(2,1)S(1)}, u32[]{:S(2)}, u32[]{:S(2)}) collective-permute-start(bf16[528,256]{1,0:T(8,128)(2,1)S(1)} %pick.7), channel_id=1, source_target_pairs={{0,2},{1,3},{2,0},{3,1},{4,6},{5,7},{6,4},{7,5},{8,10},{9,11},{10,... | collective-permute-start | bytes 811016 | tf_op jit(solution)/shard_map/ppermute | solution.py:30
  22.6 14.3 %collective-permute-start.4 = (bf16[528,256]{1,0:T(8,128)(2,1)S(1)}, bf16[528,256]{1,0:T(8,128)(2,1)S(1)}, u32[]{:S(2)}, u32[]{:S(2)}) collective-permute-start(bf16[528,256]{1,0:T(8,128)(2,1)S(1)} %collective-permute-done.3.lower_ref.upper_ref.refs_1_.refs_2_), channel_id=1, source_target_pairs={{0,4},{1,5},{2,6},{3,7},{4,8},{5,9},{6,10},{7,11},{8,12},{9,13},{1... | collective-permute-start | bytes 811016 | tf_op jit(solution)/shard_map/ppermute | solution.py:35
  23.9 20.5 %collective-permute-start.9 = (bf16[528,256]{1,0:T(8,128)(2,1)S(1)}, bf16[528,256]{1,0:T(8,128)(2,1)S(1)}, u32[]{:S(2)}, u32[]{:S(2)}) collective-permute-start(bf16[528,256]{1,0:T(8,128)(2,1)S(1)} %pick.6), channel_id=1, source_target_pairs={{0,2},{1,3},{2,0},{3,1},{4,6},{5,7},{6,4},{7,5},{8,10},{9,11},{10,... | collective-permute-start | bytes 811016 | tf_op jit(solution)/shard_map/ppermute | solution.py:30
  28.4 19.3 %collective-permute-start.8 = (bf16[528,256]{1,0:T(8,128)(2,1)S(1)}, bf16[528,256]{1,0:T(8,128)(2,1)S(1)}, u32[]{:S(2)}, u32[]{:S(2)}) collective-permute-start(bf16[528,256]{1,0:T(8,128)(2,1)S(1)} %pick.5), channel_id=1, source_target_pairs={{0,2},{1,3},{2,0},{3,1},{4,6},{5,7},{6,4},{7,5},{8,10},{9,11},{10,... | collective-permute-start | bytes 811016 | tf_op jit(solution)/shard_map/ppermute | solution.py:30
  37.0 14.5 %collective-permute-start.5 = (bf16[528,256]{1,0:T(8,128)(2,1)S(1)}, bf16[528,256]{1,0:T(8,128)(2,1)S(1)}, u32[]{:S(2)}, u32[]{:S(2)}) collective-permute-start(bf16[528,256]{1,0:T(8,128)(2,1)S(1)} %pick.4), channel_id=1, source_target_pairs={{0,2},{1,3},{2,0},{3,1},{4,6},{5,7},{6,4},{7,5},{8,10},{9,11},{10,... | collective-permute-start | bytes 811016 | tf_op jit(solution)/shard_map/ppermute | solution.py:30
  53.3 2.0 %collective-permute-start.11 = (bf16[256,1024]{1,0:T(8,128)(2,1)S(1)}, bf16[256,1024]{1,0:T(8,128)(2,1)S(1)}, u32[]{:S(2)}, u32[]{:S(2)}) collective-permute-start(bf16[256,1024]{1,0:T(8,128)(2,1)S(1)} %get-tuple-element.37), channel_id=1, source_target_pairs={{0,1},{1,0},{2,3},{3,2},{4,5},{5,4},{6,7},{7,6},{8,9},{9,8},{10,11... | collective-permute-start | bytes 1572872 | tf_op jit(solution)/shard_map/ppermute | solution.py:30

commit v2 on v1

--- a/solution.py
+++ b/solution.py
@@ -218,7 +218,7 @@
         acc_ref[tile, pair, :, at] = acc_ref[tile, pair, :, at] * fades[head] + products[head]
 
 
-def attend_kernel(sources, n_infos, first, last, *refs):
+def attend_kernel(sources, later, n_infos, first, finish, final, *refs):
     refs = list(refs)
     take = lambda n: [refs.pop(0) for _ in range(n)]
     count = len(sources)
@@ -226,10 +226,13 @@
     q_in = take(2)
     chunk_in = take(count)
     state_in = [] if first else take(3)
-    outs = take(2 if last else 3)
+    if final:
+        take(2)
+    results = take(2) if finish else []
+    state_out = [] if final else take(3)
     q_ref, chunk_ref, info_ref = take(3)
     state = acc_ref, ml_ref, best_ref = take(3)
-    buffers = take(2) if last else []
+    buffers = take(2) if finish else []
     info_sem, q_sem, chunk_sem, state_sem = take(4)
     stretch = lax.axis_index("ctx")
     pairs = acc_ref.shape[1]
@@ -243,8 +246,12 @@
     ]
     bulk = [copy_of(q_in[i], q_ref.at[i], q_sem.at[i]) for i in range(2)]
     bulk += [copy_of(chunk_in[i], chunk_ref.at[i], chunk_sem.at[i]) for i in range(count)]
-    for copy in info_copies + state_copies[::-1] + bulk:
+    bulk += state_copies[:2]
+    for copy in info_copies + state_copies[2:]:
         copy.start()
+    if not final:
+        for copy in bulk:
+            copy.start()
     if first:
         acc_ref[...] = jnp.zeros_like(acc_ref)
         ml_ref[:, :, 0] = jnp.full_like(ml_ref[:, :, 0], MASKED)
@@ -266,9 +273,11 @@
             found.append(jnp.max(best).astype(jnp.int32))
 
     second = lax.rem(lax.div(stretch, 2), 2) == 1
-    source_of = [
-        (stretch ^ bits) - jnp.where(second, upper, lower) for bits, lower, upper in sources
-    ]
+
+    def origins(table):
+        return [(stretch ^ bits) - jnp.where(second, upper, lower) for bits, lower, upper in table]
+
+    source_of = origins(sources)
 
     def view(source, tile, low_start, high_start):
         where = stretch ^ tile
@@ -279,12 +288,13 @@
         whole = (source < where) & (first_key >= high_limit)
         return seen, whole
 
-    busy = functools.reduce(
-        jnp.logical_or,
-        [view(source, tile, low[tile], high[tile])[0] for source in source_of for tile in range(2)],
-    )
-    for copy in state_copies[:2] + bulk:
-        copy.wait()
+    def any_seen(table):
+        return functools.reduce(
+            jnp.logical_or,
+            [view(source, tile, low[tile], high[tile])[0] for source in table for tile in range(2)],
+        )
+
+    busy = any_seen(source_of)
 
     def visit(step, _):
         chunk, tile = lax.div(step, 2), lax.rem(step, 2)
@@ -321,72 +331,92 @@
 
         return 0
 
+    def finished():
+        sinks = (results[0].at[:, columns(my_half(False), results[1].shape[1])], results[1])
+        leaving = []
+        for tile in (1, 0):
+            lane = lax.broadcasted_iota(jnp.int32, (1, WIDE), 1)
+            start = jnp.where(lax.rem(lane, LEN) < BLK, low[tile], high[tile])
+            active = (start >= 0) | ((stretch ^ tile) >= 1)
+            for pair in range(pairs):
+                scale = jnp.where(active, 1.0 / ml_ref[tile, pair, 1], 0.0)
+                for head in range(GROUP):
+                    lanes = slice(head * LEN, (head + 1) * LEN)
+                    blended = (acc_ref[tile, pair, :, lanes] * scale[:, lanes]).astype(jnp.bfloat16)
+                    at = (pair * GROUP + head) * HD
+                    buffers[tile][:, at : at + HD] = blended.T
+            copy = copy_of(buffers[tile], sinks[tile], q_sem.at[tile])
+            copy.start()
+            leaving.append(copy)
+        for copy in leaving:
+            copy.wait()
+
+    if final:
+
+        @pl.when(busy)
+        def _():
+            for copy in bulk:
+                copy.start()
+            for copy in bulk:
+                copy.wait()
+            lax.fori_loop(0, 2 * count, visit, 0)
+            finished()
+
+        return
+
+    for copy in bulk:
+        copy.wait()
+
     @pl.when(busy)
     def _():
         lax.fori_loop(0, 2 * count, visit, 0)
 
-    if not last:
-        back = [
-            copy_of(source, target, state_sem.at[i]) for i, (source, target) in enumerate(zip(state, outs))
-        ]
-        back[2].start()
-
-        @pl.when(busy | first)
-        def _():
-            for copy in back[:2]:
-                copy.start()
-            for copy in back[:2]:
-                copy.wait()
-
-        back[2].wait()
-        return
-
-    sinks = (outs[0].at[:, columns(my_half(False), outs[1].shape[1])], outs[1])
-    leaving = []
-    for tile in (1, 0):
-        lane = lax.broadcasted_iota(jnp.int32, (1, WIDE), 1)
-        start = jnp.where(lax.rem(lane, LEN) < BLK, low[tile], high[tile])
-        active = (start >= 0) | ((stretch ^ tile) >= 1)
-        for pair in range(pairs):
-            scale = jnp.where(active, 1.0 / ml_ref[tile, pair, 1], 0.0)
-            for head in range(GROUP):
-                lanes = slice(head * LEN, (head + 1) * LEN)
-                blended = (acc_ref[tile, pair, :, lanes] * scale[:, lanes]).astype(jnp.bfloat16)
-                at = (pair * GROUP + head) * HD
-                buffers[tile][:, at : at + HD] = blended.T
-        copy = copy_of(buffers[tile], sinks[tile], q_sem.at[tile])
-        copy.start()
-        leaving.append(copy)
-    for copy in leaving:
-        copy.wait()
-
-
-def attend(infos, qs, chunks, sources, state, width=0):
-    last = width > 0
-    first = state is None
+    back = [
+        copy_of(source, target, state_sem.at[i]) for i, (source, target) in enumerate(zip(state, state_out))
+    ]
+    back[2].start()
+    back[2].wait()
+    goes_on = any_seen(origins(later)) if finish else True
+
+    @pl.when((busy | first) & goes_on)
+    def _():
+        for copy in back[:2]:
+            copy.start()
+        for copy in back[:2]:
+            copy.wait()
+
+    if finish:
+        pl.when(jnp.logical_not(goes_on))(finished)
+
+
+def attend(infos, qs, chunks, sources, state, later=None, results=None, width=0):
+    finish, final, first = width > 0, results is not None, state is None
     pairs = qs[0].shape[0]
     args = list(infos) + list(qs) + list(chunks)
     state_shapes = (2, pairs, HD, WIDE), (2, pairs, 2, 1, WIDE), (4, 1, HD)
+    half = pairs * GROUP * HD
+    shapes = [jax.ShapeDtypeStruct((LEN, w), jnp.bfloat16) for w in (width, half)] if finish else []
     aliases = {}
     if not first:
-        if not last:
-            aliases = {len(args) + i: i for i in range(3)}
+        if not final:
+            aliases = {len(args) + i: len(shapes) + i for i in range(3)}
         args += list(state)
+    if final:
+        aliases = {len(args) + i: i for i in range(2)}
+        args += list(results)
+    else:
+        shapes += [jax.ShapeDtypeStruct(s, jnp.float32) for s in state_shapes]
     scratch = [
         pltpu.VMEM((2,) + qs[0].shape, jnp.bfloat16),
         pltpu.VMEM((len(chunks),) + CHUNK, jnp.bfloat16),
         pltpu.VMEM((max(len(infos), 1), 16, LEN), jnp.bfloat16),
     ] + [pltpu.VMEM(s, jnp.float32) for s in state_shapes]
-    if last:
-        half = pairs * GROUP * HD
-        shapes = [jax.ShapeDtypeStruct((LEN, w), jnp.bfloat16) for w in (width, half)]
+    if finish:
         scratch += [pltpu.VMEM((LEN, half), jnp.bfloat16)] * 2
-    else:
-        shapes = [jax.ShapeDtypeStruct(s, jnp.float32) for s in state_shapes]
     scratch += [pltpu.SemaphoreType.DMA((n,)) for n in (max(len(infos), 1), 2, len(chunks), 3)]
     elements = len(chunks) * 2 * pairs * LEN * WIDE
     return pl.pallas_call(
-        functools.partial(attend_kernel, sources, len(infos), first, last),
+        functools.partial(attend_kernel, sources, later, len(infos), first, finish, final),
         out_shape=shapes,
         in_specs=[ANY] * len(args),
         out_specs=[ANY] * len(shapes),
@@ -414,22 +444,27 @@
     a_pair = shifted(pair, 4)
     x_own = crossed(own, a_own)
     b_own = shifted(a_own, 4)
-    state = attend((own, pair), qs, (own, pair), ((0, 0, 0), (1, 0, 0)), None)
+    state = attend((own, pair), qs, (own,), ((0, 0, 0),), None)
     x_pair = crossed(pair, a_pair)
     b_pair = shifted(a_pair, 4)
-    state = attend((a_own, a_pair, x_own), qs, (a_own,), ((0, 4, 4),), state)
+    state = attend(
+        (a_own, a_pair, x_own), qs, (pair, a_own), ((1, 0, 0), (0, 4, 4)), state
+    )
     xb_own = crossed(a_own, b_own)
     state = attend((), qs, (a_pair, x_own), ((1, 4, 4), (2, 4, 0)), state)
     xb_pair = crossed(a_pair, b_pair)
     state = attend((), qs, (x_pair,), ((3, 4, 0),), state)
-    state = attend(
+    rest = ((3, 8, 4),)
+    full, out_send, *state = attend(
         (b_own, b_pair, xb_own),
         qs,
         (b_own, b_pair, xb_own),
         ((0, 8, 8), (1, 8, 8), (2, 8, 4)),
         state,
+        later=rest,
+        width=width,
     )
-    full, out_send = attend((), qs, (xb_pair,), ((3, 8, 4),), state, width)
+    full, out_send = attend((), qs, (xb_pair,), rest, state, results=(full, out_send), width=width)
     return merge(exchanged(out_send, 1), full)
 
 

time: 56.3 us -> 55.9 us (level)
  transfers between devices with their start and end apart: 12 -> 12, of which waited for: 5 -> 5; matrix products, arithmetic and copies ran while one was open for 0% -> 0% of each run, Pallas kernels for 42% -> 45%
where the time goes in v2:
time: 55.9 us; the launch traced here: 55.7 us
  Pallas kernels  27.6 us (49%)
  waiting for transfers between devices  17.2 us (31%)
  starting transfers between devices  9.25 us (17%)
  local copies, waits for them, and re-layouts  1.48 us (3%)
    pallas_call x6, Pallas kernels, attend(): pl.pallas_call(functools.partial(attend_kernel, sources, later, len(infos...  22.5 us
    ppermute x4, waiting for transfers between devices, shifted(): return lax.ppermute(x, 'ctx', [(i, (i + distance) % n) for i in range(n)])  13.3 us
    ppermute x8, starting transfers between devices, exchanged(): return lax.ppermute(x, 'ctx', [(i, i ^ bit) for i in range(n)])  5.31 us
    ppermute x4, starting transfers between devices, shifted(): return lax.ppermute(x, 'ctx', [(i, (i + distance) % n) for i in range(n)])  3.94 us
    ppermute x8, waiting for transfers between devices, exchanged(): return lax.ppermute(x, 'ctx', [(i, i ^ bit) for i in range(n)])  3.9 us
    pallas_call x2, Pallas kernels, prep_kv(): pl.pallas_call(functools.partial(prep_kv_kernel, other, len(tables)), out...  3.52 us
    unnamed x8, local copies, waits for them, and re-layouts  1.48 us
  transfers between devices with their start and end apart: 12, of which 5 were waited for; matrix products, arithmetic and copies ran while one was open for 0% of the time, Pallas kernels for 45%

profile of v2, /device:TPU:23, one launch (start us, length us, event | category | flops | bytes accessed | tf_op | source)
XLA Modules:
  0.0 55.7 jit_solution(2283456097801060325)
XLA Ops:
  0.2 2.3 %collective-permute-done.1.refs_1_ = s32[1,2]{1,0:T(1,128)S(1)} collective-permute-done((s32[1,2]{1,0:T(1,128)}, s32[1,2]{1,0:T(1,128)S(1)}, u32[]{:S(2)}, u32[]{:S(2)}) %collective-permute-start.1) | collective-permute-done | bytes 40 | tf_op jit(solution)/shard_map/ppermute | solution.py:30
  2.6 0.5 copy-done.3
  3.1 1.8 %prep_kv.2 = bf16[528,256]{1,0:T(8,128)(2,1)} custom-call(bf16[256,512]{1,0:T(8,128)(2,1)} %k_ref.3, bf16[256,512]{1,0:T(8,128)(2,1)} %v_ref.3, s32[1,2]{1,0:T(1,128)} %refs_0_.3, s32[1,2]{1,0:T(1,128)} %copy-done.3), custom_call_target="tpu_custom_call" | custom-call | tf_op jit(solution)/shard_map/prep_kv/pallas_call | solution.py:95
  4.9 1.9 %collective-permute-start.2 = (bf16[528,256]{1,0:T(8,128)(2,1)}, bf16[528,256]{1,0:T(8,128)(2,1)S(1)}, u32[]{:S(2)}, u32[]{:S(2)}) collective-permute-start(bf16[528,256]{1,0:T(8,128)(2,1)} %prep_kv.2), channel_id=1, source_target_pairs={{0,1},{1,0},{2,3},{3,2},{4,5},{5,4},{6,7},{7,6},{8,9},{9,8},{10,11... | collective-permute-start | bytes 811016 | tf_op jit(solution)/shard_map/ppermute | solution.py:30
  6.7 1.8 %prep_kv.3.lower_ref.refs_0_.refs_4_ = bf16[528,256]{1,0:T(8,128)(2,1)} custom-call(bf16[256,512]{1,0:T(8,128)(2,1)} %k_ref.3, bf16[256,512]{1,0:T(8,128)(2,1)} %v_ref.3, s32[1,2]{1,0:T(1,128)} %refs_0_.3), custom_call_target="tpu_custom_call" | custom-call | tf_op jit(solution)/shard_map/prep_kv/pallas_call | solution.py:95
  8.5 1.3 %collective-permute-start.6 = (bf16[528,256]{1,0:T(8,128)(2,1)}, bf16[528,256]{1,0:T(8,128)(2,1)S(1)}, u32[]{:S(2)}, u32[]{:S(2)}) collective-permute-start(bf16[528,256]{1,0:T(8,128)(2,1)} %prep_kv.3.lower_ref.refs_0_.refs_4_), channel_id=1, source_target_pairs={{0,4},{1,5},{2,6},{3,7},{4,8},{5,9},{6,10},{7,11},{8,12},{9,13},{1... | collective-permute-start | bytes 811016 | tf_op jit(solution)/shard_map/ppermute | solution.py:35
  9.9 0.3 prep_q.3
  10.2 0.4 collective-permute-start
  10.6 6.2 %collective-permute-done.6.lower_ref.upper_ref.refs_0_.refs_6_ = bf16[528,256]{1,0:T(8,128)(2,1)S(1)} collective-permute-done((bf16[528,256]{1,0:T(8,128)(2,1)}, bf16[528,256]{1,0:T(8,128)(2,1)S(1)}, u32[]{:S(2)}, u32[]{:S(2)}) %collective-permute-start.6) | collective-permute-done | bytes 270368 | tf_op jit(solution)/shard_map/ppermute | solution.py:35
  16.8 1.3 %collective-permute-start.7 = (bf16[528,256]{1,0:T(8,128)(2,1)S(1)}, bf16[528,256]{1,0:T(8,128)(2,1)S(1)}, u32[]{:S(2)}, u32[]{:S(2)}) collective-permute-start(bf16[528,256]{1,0:T(8,128)(2,1)S(1)} %collective-permute-done.6.lower_ref.upper_ref.refs_0_.refs_6_), channel_id=1, source_target_pairs={{0,4},{1,5},{2,6},{3,7},{4,8},{5,9},{6,10},{7,11},{8,12},{9,13},{1... | collective-permute-start | bytes 811016 | tf_op jit(solution)/shard_map/ppermute | solution.py:35
  18.1 1.0 %copy-done.1 = bf16[528,256]{1,0:T(8,128)(2,1)S(1)} copy-done((bf16[528,256]{1,0:T(8,128)(2,1)S(1)}, bf16[528,256]{1,0:T(8,128)(2,1)}, u32[]{:S(2)}) %copy-start.1) | copy-done | bytes 270360
  19.4 3.2 %collective-permute-done.3.lower_ref.upper_ref.refs_1_.refs_2_ = bf16[528,256]{1,0:T(8,128)(2,1)S(1)} collective-permute-done((bf16[528,256]{1,0:T(8,128)(2,1)S(1)}, bf16[528,256]{1,0:T(8,128)(2,1)S(1)}, u32[]{:S(2)}, u32[]{:S(2)}) %collective-permute-start.3) | collective-permute-done | bytes 270368 | tf_op jit(solution)/shard_map/ppermute | solution.py:35
  22.6 1.3 %collective-permute-start.4 = (bf16[528,256]{1,0:T(8,128)(2,1)S(1)}, bf16[528,256]{1,0:T(8,128)(2,1)S(1)}, u32[]{:S(2)}, u32[]{:S(2)}) collective-permute-start(bf16[528,256]{1,0:T(8,128)(2,1)S(1)} %collective-permute-done.3.lower_ref.upper_ref.refs_1_.refs_2_), channel_id=1, source_target_pairs={{0,4},{1,5},{2,6},{3,7},{4,8},{5,9},{6,10},{7,11},{8,12},{9,13},{1... | collective-permute-start | bytes 811016 | tf_op jit(solution)/shard_map/ppermute | solution.py:35
  24.2 0.3 prep_q.2.refs_2_.refs_3_.refs_0_
  24.5 3.9 %collective-permute-done.7.upper_ref.refs_0_.refs_5_ = bf16[528,256]{1,0:T(8,128)(2,1)S(1)} collective-permute-done((bf16[528,256]{1,0:T(8,128)(2,1)S(1)}, bf16[528,256]{1,0:T(8,128)(2,1)S(1)}, u32[]{:S(2)}, u32[]{:S(2)}) %collective-permute-start.7) | collective-permute-done | bytes 270368 | tf_op jit(solution)/shard_map/ppermute | solution.py:35
  28.7 2.1 %attend.6 = (f32[2,2,128,1024]{3,2,1,0:T(8,128)S(1)}, f32[2,2,2,1,1024]{4,3,2,1,0:T(1,128)S(1)}, f32[4,1,128]{2,1,0:T(1,128)S(1)}) custom-call(bf16[528,256]{1,0:T(8,128)(2,1)S(1)} %copy-done.2, bf16[528,256]{1,0:T(8,128)(2,1)S(1)} %collective-permute-done.2.lower_ref.refs_1_.refs_5_, bf16[2,128,1024]{2,1,0:T(8,128)(2,1)S(1)} %prep_q.2.refs_2_.refs_3_.refs_0_, ...), custom_call_target="tpu_custom_call" | custom-call | flops 536870912 | bytes 6291456 | tf_op jit(solution)/shard_map/attend/pallas_call | solution.py:418
  30.8 6.1 %attend.7 = (f32[2,2,128,1024]{3,2,1,0:T(8,128)S(1)}, f32[2,2,2,1,1024]{4,3,2,1,0:T(1,128)S(1)}, f32[4,1,128]{2,1,0:T(1,128)S(1)}) custom-call(bf16[528,256]{1,0:T(8,128)(2,1)S(1)} %collective-permute-done.6.lower_ref.upper_ref.refs_0_.refs_6_, ...), custom_call_target="tpu_custom_call", output_to_operand_aliasing={{0}: (7, {}), {1}: (8, {}), {2}: (9, {})} | custom-call | flops 1073741824 | bytes 6291456 | tf_op jit(solution)/shard_map/attend/pallas_call | solution.py:418
  37.0 1.5 %collective-permute-start.5 = (bf16[528,256]{1,0:T(8,128)(2,1)S(1)}, bf16[528,256]{1,0:T(8,128)(2,1)S(1)}, u32[]{:S(2)}, u32[]{:S(2)}) collective-permute-start(bf16[528,256]{1,0:T(8,128)(2,1)S(1)} %pick.4), channel_id=1, source_target_pairs={{0,2},{1,3},{2,0},{3,1},{4,6},{5,7},{6,4},{7,5},{8,10},{9,11},{10,... | collective-permute-start | bytes 811016 | tf_op jit(solution)/shard_map/ppermute | solution.py:30
  38.6 5.9 %attend.8 = (f32[2,2,128,1024]{3,2,1,0:T(8,128)S(1)}, f32[2,2,2,1,1024]{4,3,2,1,0:T(1,128)S(1)}, f32[4,1,128]{2,1,0:T(1,128)S(1)}) custom-call(bf16[2,128,1024]{2,1,0:T(8,128)(2,1)S(1)} %prep_q.2.refs_2_.refs_3_.refs_0_, ...), custom_call_target="tpu_custom_call", output_to_operand_aliasing={{0}: (4, {}), {1}: (5, {}), {2}: (6, {})} | custom-call | flops 1073741824 | bytes 6291456 | tf_op jit(solution)/shard_map/attend/pallas_call | solution.py:418
  44.5 3.3 %attend.9 = (f32[2,2,128,1024]{3,2,1,0:T(8,128)S(1)}, f32[2,2,2,1,1024]{4,3,2,1,0:T(1,128)S(1)}, f32[4,1,128]{2,1,0:T(1,128)S(1)}) custom-call(bf16[2,128,1024]{2,1,0:T(8,128)(2,1)S(1)} %prep_q.2.refs_2_.refs_3_.refs_0_, ...), custom_call_target="tpu_custom_call", output_to_operand_aliasing={{0}: (3, {}), {1}: (4, {}), {2}: (5, {})} | custom-call | flops 536870912 | bytes 6291456 | tf_op jit(solution)/shard_map/attend/pallas_call | solution.py:418
  47.8 4.9 %attend.10 = (bf16[256,2048]{1,0:T(8,128)(2,1)}, bf16[256,1024]{1,0:T(8,128)(2,1)S(1)}, f32[2,2,128,1024]{3,2,1,0:T(8,128)S(1)}, f32[2,2,2,1,1024]{4,3,2,1,0:T(1,128)S(1)}, f32[4,1,128]{2,1,0:T(1,128)S(1)}) custom-call(bf16[528,256]{1,0:T(8,128)(2,1)S(1)} %collective-permute-done.7.upper_ref.refs_0_.refs_, ...), custom_call_target="tpu_custom_call", output_to_operand_aliasing={{2}: (8, {}), {3}: (9, {}), {4}: (10, {})} | custom-call | flops 1610612736 | bytes 6291456 | tf_op jit(solution)/shard_map/attend/pallas_call | solution.py:418
  52.9 0.4 collective-permute-start.11
  53.3 1.6 %collective-permute-done.11.got_ref = bf16[256,1024]{1,0:T(8,128)(2,1)S(1)} collective-permute-done((bf16[256,1024]{1,0:T(8,128)(2,1)S(1)}, bf16[256,1024]{1,0:T(8,128)(2,1)S(1)}, u32[]{:S(2)}, u32[]{:S(2)}) %collective-permute-start.11) | collective-permute-done | bytes 524320 | tf_op jit(solution)/shard_map/ppermute | solution.py:30
  54.9 0.8 %merge.1 = bf16[256,2048]{1,0:T(8,128)(2,1)} custom-call(bf16[256,1024]{1,0:T(8,128)(2,1)S(1)} %collective-permute-done.11.got_ref, bf16[256,2048]{1,0:T(8,128)(2,1)} %get-tuple-element.42.full_in), custom_call_target="tpu_custom_call", output_to_operand_aliasing={{}: (1, {})} | custom-call | tf_op jit(solution)/shard_map/merge/pallas_call | solution.py:182
  (23 shorter events, 1.5 us)
Async XLA Ops:
  0.0 9.9 %copy-start = (bf16[256,2048]{1,0:T(8,128)(2,1)S(1)}, bf16[256,2048]{1,0:T(8,128)(2,1)}, u32[]{:S(2)}) copy-start(bf16[256,2048]{1,0:T(8,128)(2,1)} %q_ref.3) | copy-start | bytes 3145732
  0.0 2.6 %collective-permute-start.1 = (s32[1,2]{1,0:T(1,128)}, s32[1,2]{1,0:T(1,128)S(1)}, u32[]{:S(2)}, u32[]{:S(2)}) collective-permute-start(s32[1,2]{1,0:T(1,128)} %refs_0_.3), channel_id=1, source_target_pairs={{0,2},{1,3},{2,0},{3,1},{4,6},{5,7},{6,4},{7,5},{8,10},{9,11},{10,... | collective-permute-start | bytes 32 | tf_op jit(solution)/shard_map/ppermute | solution.py:30
  2.6 0.5 copy-start.3
  4.9 5.7 %collective-permute-start.2 = (bf16[528,256]{1,0:T(8,128)(2,1)}, bf16[528,256]{1,0:T(8,128)(2,1)S(1)}, u32[]{:S(2)}, u32[]{:S(2)}) collective-permute-start(bf16[528,256]{1,0:T(8,128)(2,1)} %prep_kv.2), channel_id=1, source_target_pairs={{0,1},{1,0},{2,3},{3,2},{4,5},{5,4},{6,7},{7,6},{8,9},{9,8},{10,11... | collective-permute-start | bytes 811016 | tf_op jit(solution)/shard_map/ppermute | solution.py:30
  8.5 8.3 %collective-permute-start.6 = (bf16[528,256]{1,0:T(8,128)(2,1)}, bf16[528,256]{1,0:T(8,128)(2,1)S(1)}, u32[]{:S(2)}, u32[]{:S(2)}) collective-permute-start(bf16[528,256]{1,0:T(8,128)(2,1)} %prep_kv.3.lower_ref.refs_0_.refs_4_), channel_id=1, source_target_pairs={{0,4},{1,5},{2,6},{3,7},{4,8},{5,9},{6,10},{7,11},{8,12},{9,13},{1... | collective-permute-start | bytes 811016 | tf_op jit(solution)/shard_map/ppermute | solution.py:35
  9.9 18.9 %copy-start.2 = (bf16[528,256]{1,0:T(8,128)(2,1)S(1)}, bf16[528,256]{1,0:T(8,128)(2,1)}, u32[]{:S(2)}) copy-start(bf16[528,256]{1,0:T(8,128)(2,1)} %prep_kv.3.lower_ref.refs_0_.refs_4_) | copy-start | bytes 811012
  10.2 18.5 %collective-permute-start = (bf16[2,128,1024]{2,1,0:T(8,128)(2,1)S(1)}, bf16[2,128,1024]{2,1,0:T(8,128)(2,1)S(1)}, u32[]{:S(2)}, u32[]{:S(2)}) collective-permute-start(bf16[2,128,1024]{2,1,0:T(8,128)(2,1)S(1)} %prep_q.3), channel_id=1, source_target_pairs={{0,1},{1,0},{2,3},{3,2},{4,5},{5,4},{6,7},{7,6},{8,9},{9,8},{10,11... | collective-permute-start | bytes 1572872 | tf_op jit(solution)/shard_map/ppermute | solution.py:30
  10.5 12.0 %collective-permute-start.3 = (bf16[528,256]{1,0:T(8,128)(2,1)S(1)}, bf16[528,256]{1,0:T(8,128)(2,1)S(1)}, u32[]{:S(2)}, u32[]{:S(2)}) collective-permute-start(bf16[528,256]{1,0:T(8,128)(2,1)S(1)} %collective-permute-done.2.lower_ref.refs_1_.refs_5_), channel_id=1, source_target_pairs={{0,4},{1,5},{2,6},{3,7},{4,8},{5,9},{6,10},{7,11},{8,12},{9,13},{1... | collective-permute-start | bytes 811016 | tf_op jit(solution)/shard_map/ppermute | solution.py:35
  16.8 11.6 %collective-permute-start.7 = (bf16[528,256]{1,0:T(8,128)(2,1)S(1)}, bf16[528,256]{1,0:T(8,128)(2,1)S(1)}, u32[]{:S(2)}, u32[]{:S(2)}) collective-permute-start(bf16[528,256]{1,0:T(8,128)(2,1)S(1)} %collective-permute-done.6.lower_ref.upper_ref.refs_0_.refs_6_), channel_id=1, source_target_pairs={{0,4},{1,5},{2,6},{3,7},{4,8},{5,9},{6,10},{7,11},{8,12},{9,13},{1... | collective-permute-start | bytes 811016 | tf_op jit(solution)/shard_map/ppermute | solution.py:35
  18.1 1.0 %copy-start.1 = (bf16[528,256]{1,0:T(8,128)(2,1)S(1)}, bf16[528,256]{1,0:T(8,128)(2,1)}, u32[]{:S(2)}) copy-start(bf16[528,256]{1,0:T(8,128)(2,1)} %prep_kv.3.lower_ref.refs_0_.refs_4_) | copy-start | bytes 811012
  19.1 11.7 %collective-permute-start.10 = (bf16[528,256]{1,0:T(8,128)(2,1)S(1)}, bf16[528,256]{1,0:T(8,128)(2,1)S(1)}, u32[]{:S(2)}, u32[]{:S(2)}) collective-permute-start(bf16[528,256]{1,0:T(8,128)(2,1)S(1)} %pick.7), channel_id=1, source_target_pairs={{0,2},{1,3},{2,0},{3,1},{4,6},{5,7},{6,4},{7,5},{8,10},{9,11},{10,... | collective-permute-start | bytes 811016 | tf_op jit(solution)/shard_map/ppermute | solution.py:30
  22.6 14.4 %collective-permute-start.4 = (bf16[528,256]{1,0:T(8,128)(2,1)S(1)}, bf16[528,256]{1,0:T(8,128)(2,1)S(1)}, u32[]{:S(2)}, u32[]{:S(2)}) collective-permute-start(bf16[528,256]{1,0:T(8,128)(2,1)S(1)} %collective-permute-done.3.lower_ref.upper_ref.refs_1_.refs_2_), channel_id=1, source_target_pairs={{0,4},{1,5},{2,6},{3,7},{4,8},{5,9},{6,10},{7,11},{8,12},{9,13},{1... | collective-permute-start | bytes 811016 | tf_op jit(solution)/shard_map/ppermute | solution.py:35
  23.9 20.6 %collective-permute-start.9 = (bf16[528,256]{1,0:T(8,128)(2,1)S(1)}, bf16[528,256]{1,0:T(8,128)(2,1)S(1)}, u32[]{:S(2)}, u32[]{:S(2)}) collective-permute-start(bf16[528,256]{1,0:T(8,128)(2,1)S(1)} %pick.6), channel_id=1, source_target_pairs={{0,2},{1,3},{2,0},{3,1},{4,6},{5,7},{6,4},{7,5},{8,10},{9,11},{10,... | collective-permute-start | bytes 811016 | tf_op jit(solution)/shard_map/ppermute | solution.py:30
  28.4 19.4 %collective-permute-start.8 = (bf16[528,256]{1,0:T(8,128)(2,1)S(1)}, bf16[528,256]{1,0:T(8,128)(2,1)S(1)}, u32[]{:S(2)}, u32[]{:S(2)}) collective-permute-start(bf16[528,256]{1,0:T(8,128)(2,1)S(1)} %pick.5), channel_id=1, source_target_pairs={{0,2},{1,3},{2,0},{3,1},{4,6},{5,7},{6,4},{7,5},{8,10},{9,11},{10,... | collective-permute-start | bytes 811016 | tf_op jit(solution)/shard_map/ppermute | solution.py:30
  37.0 15.7 %collective-permute-start.5 = (bf16[528,256]{1,0:T(8,128)(2,1)S(1)}, bf16[528,256]{1,0:T(8,128)(2,1)S(1)}, u32[]{:S(2)}, u32[]{:S(2)}) collective-permute-start(bf16[528,256]{1,0:T(8,128)(2,1)S(1)} %pick.4), channel_id=1, source_target_pairs={{0,2},{1,3},{2,0},{3,1},{4,6},{5,7},{6,4},{7,5},{8,10},{9,11},{10,... | collective-permute-start | bytes 811016 | tf_op jit(solution)/shard_map/ppermute | solution.py:30
  52.9 2.0 %collective-permute-start.11 = (bf16[256,1024]{1,0:T(8,128)(2,1)S(1)}, bf16[256,1024]{1,0:T(8,128)(2,1)S(1)}, u32[]{:S(2)}, u32[]{:S(2)}) collective-permute-start(bf16[256,1024]{1,0:T(8,128)(2,1)S(1)} %get-tuple-element.41), channel_id=1, source_target_pairs={{0,1},{1,0},{2,3},{3,2},{4,5},{5,4},{6,7},{7,6},{8,9},{9,8},{10,11... | collective-permute-start | bytes 1572872 | tf_op jit(solution)/shard_map/ppermute | solution.py:30

commit v3 on v2

--- a/solution.py
+++ b/solution.py
@@ -23,6 +23,8 @@
 SMEM = pl.BlockSpec(memory_space=pltpu.SMEM)
 ANY = pl.BlockSpec(memory_space=pl.ANY)
 LIMIT = 20 << 20
+SMALL = pltpu.CompilerParams(vmem_limit_bytes=4 << 20)
+BOTH = (0, 1)
 
 
 def exchanged(x, bit):
@@ -33,6 +35,10 @@
 def shifted(x, distance):
     n = lax.axis_size("ctx")
     return lax.ppermute(x, "ctx", [(i, (i + distance) % n) for i in range(n)])
+
+
+def in_hbm(x):
+    return pltpu.with_memory_space_constraint(x, pltpu.HBM)
 
 
 def my_half(other):
@@ -106,8 +112,9 @@
             pltpu.SemaphoreType.DMA((4 + len(tables),)),
             pltpu.SemaphoreType.DMA((4,)),
         ],
+        compiler_params=SMALL,
         name="prep_kv",
-    )(keys, values, *tables)
+    )(in_hbm(keys), in_hbm(values), *tables)
 
 
 def prep_q_kernel(other, q_ref, out_ref, q_buf, sems):
@@ -140,9 +147,9 @@
             pltpu.VMEM((pairs, LEN, GROUP * HD), jnp.bfloat16),
             pltpu.SemaphoreType.DMA((pairs,)),
         ],
-        compiler_params=pltpu.CompilerParams(vmem_limit_bytes=4 << 20),
+        compiler_params=SMALL,
         name="prep_q",
-    )(queries)
+    )(in_hbm(queries))
 
 
 def pick_kernel(lower_ref, upper_ref, out_ref, sem):
@@ -186,7 +193,7 @@
         out_specs=ANY,
         scratch_shapes=[pltpu.SemaphoreType.DMA],
         input_output_aliases={1: 0},
-        compiler_params=pltpu.CompilerParams(vmem_limit_bytes=4 << 20),
+        compiler_params=SMALL,
         name="merge",
     )(got, full)
 
@@ -275,7 +282,7 @@
     second = lax.rem(lax.div(stretch, 2), 2) == 1
 
     def origins(table):
-        return [(stretch ^ bits) - jnp.where(second, upper, lower) for bits, lower, upper in table]
+        return [(stretch ^ bits) - jnp.where(second, upper, lower) for bits, lower, upper, *_ in table]
 
     source_of = origins(sources)
 
@@ -304,6 +311,9 @@
         low_start = jnp.where(tile == 0, low[0], low[1])
         high_start = jnp.where(tile == 0, high[0], high[1])
         seen, whole = view(source, tile, low_start, high_start)
+        for i, (*_, tiles) in enumerate(sources):
+            for left_out in set(range(2)) - set(tiles):
+                seen &= jnp.logical_not((chunk == i) & (tile == left_out))
 
         def all_heads(masked):
             bounds = None
@@ -433,33 +443,35 @@
 def steps(queries, keys, values, doc_starts):
     rows, width = queries.shape
     assert rows == LEN and keys.shape[1] == 4 * HD and lax.axis_size("ctx") % 4 == 0
-    own = prep_kv(keys, values, (doc_starts,), False)
+    own = prep_kv(keys, values, (in_hbm(doc_starts),), False)
     a_own = shifted(own, 4)
     across = exchanged(doc_starts, 2)
     q_send = prep_q(queries, True)
     q_pair = exchanged(q_send, 1)
-    send = prep_kv(keys, values, (doc_starts, across), True)
+    send = prep_kv(keys, values, (in_hbm(doc_starts), across), True)
     pair = exchanged(send, 1)
     qs = (prep_q(queries, False), q_pair)
     a_pair = shifted(pair, 4)
     x_own = crossed(own, a_own)
     b_own = shifted(a_own, 4)
-    state = attend((own, pair), qs, (own,), ((0, 0, 0),), None)
+    state = attend(
+        (own, pair), qs, (own, pair), ((0, 0, 0, BOTH), (1, 0, 0, (0,))), None
+    )
     x_pair = crossed(pair, a_pair)
     b_pair = shifted(a_pair, 4)
     state = attend(
-        (a_own, a_pair, x_own), qs, (pair, a_own), ((1, 0, 0), (0, 4, 4)), state
+        (a_own, a_pair, x_own), qs, (pair, a_own), ((1, 0, 0, (1,)), (0, 4, 4, BOTH)), state
     )
     xb_own = crossed(a_own, b_own)
-    state = attend((), qs, (a_pair, x_own), ((1, 4, 4), (2, 4, 0)), state)
+    state = attend((), qs, (a_pair, x_own), ((1, 4, 4, BOTH), (2, 4, 0, BOTH)), state)
     xb_pair = crossed(a_pair, b_pair)
-    state = attend((), qs, (x_pair,), ((3, 4, 0),), state)
-    rest = ((3, 8, 4),)
+    state = attend((), qs, (x_pair,), ((3, 4, 0, BOTH),), state)
+    rest = ((3, 8, 4, BOTH),)
     full, out_send, *state = attend(
         (b_own, b_pair, xb_own),
         qs,
         (b_own, b_pair, xb_own),
-        ((0, 8, 8), (1, 8, 8), (2, 8, 4)),
+        ((0, 8, 8, BOTH), (1, 8, 8, BOTH), (2, 8, 4, BOTH)),
         state,
         later=rest,
         width=width,

time: 55.9 us -> 56.2 us (level)
  local copies, waits for them, and re-layouts: 1.48 us -> 0 us
  starting transfers between devices: 9.25 us -> 10.5 us
  Pallas kernels: 27.6 us -> 28.8 us
  waiting for transfers between devices: 17.2 us -> 16.4 us
    pallas_call x2, Pallas kernels: 0.61 us -> 2.42 us  [prep_q(): pl.pallas_call(functools.partial(prep_q_kernel, other), out_shape=jax.Sha...]
    unnamed x8 -> x0, local copies, waits for them, and re-layouts: 1.48 us -> none
    ppermute x8, starting transfers between devices: 5.31 us -> 6.61 us  [exchanged(): return lax.ppermute(x, 'ctx', [(i, i ^ bit) for i in range(n)])]
    ppermute x4, waiting for transfers between devices: 13.3 us -> 12.6 us  [shifted(): return lax.ppermute(x, 'ctx', [(i, (i + distance) % n) for i in range(n)])]
    pallas_call x2, Pallas kernels: 3.52 us -> 2.81 us  [prep_kv(): pl.pallas_call(functools.partial(prep_kv_kernel, other, len(tables)), out...]
  transfers between devices with their start and end apart: 12 -> 12, of which waited for: 5 -> 5; matrix products, arithmetic and copies ran while one was open for 0% -> 0% of each run, Pallas kernels for 45% -> 47%
where the time goes in v3:
time: 56.2 us; the launch traced here: 55.9 us
  Pallas kernels  28.8 us (51%)
  waiting for transfers between devices  16.4 us (29%)
  starting transfers between devices  10.5 us (19%)
    pallas_call x6, Pallas kernels, attend(): pl.pallas_call(functools.partial(attend_kernel, sources, later, len(infos...  22.6 us
    ppermute x4, waiting for transfers between devices, shifted(): return lax.ppermute(x, 'ctx', [(i, (i + distance) % n) for i in range(n)])  12.6 us
    ppermute x8, starting transfers between devices, exchanged(): return lax.ppermute(x, 'ctx', [(i, i ^ bit) for i in range(n)])  6.61 us
    ppermute x4, starting transfers between devices, shifted(): return lax.ppermute(x, 'ctx', [(i, (i + distance) % n) for i in range(n)])  3.94 us
    ppermute x8, waiting for transfers between devices, exchanged(): return lax.ppermute(x, 'ctx', [(i, i ^ bit) for i in range(n)])  3.88 us
    pallas_call x2, Pallas kernels, prep_kv(): pl.pallas_call(functools.partial(prep_kv_kernel, other, len(tables)), out...  2.81 us
    pallas_call x2, Pallas kernels, prep_q(): pl.pallas_call(functools.partial(prep_q_kernel, other), out_shape=jax.Sha...  2.42 us
  transfers between devices with their start and end apart: 12, of which 5 were waited for; matrix products, arithmetic and copies ran while one was open for 0% of the time, Pallas kernels for 47%

profile of v3, /device:TPU:23, one launch (start us, length us, event | category | flops | bytes accessed | tf_op | source)
XLA Modules:
  0.0 55.9 jit_solution(6678717515672393942)
XLA Ops:
  0.2 2.3 %collective-permute-done.1.refs_1_ = s32[1,2]{1,0:T(1,128)S(1)} collective-permute-done((s32[1,2]{1,0:T(1,128)}, s32[1,2]{1,0:T(1,128)S(1)}, u32[]{:S(2)}, u32[]{:S(2)}) %collective-permute-start.1) | collective-permute-done | bytes 40 | tf_op jit(solution)/shard_map/ppermute | solution.py:32
  2.6 1.4 %prep_kv.2 = bf16[528,256]{1,0:T(8,128)(2,1)S(1)} custom-call(bf16[256,512]{1,0:T(8,128)(2,1)} %k_ref.3, bf16[256,512]{1,0:T(8,128)(2,1)} %v_ref.3, s32[1,2]{1,0:T(1,128)} %refs_0_.3, s32[1,2]{1,0:T(1,128)S(1)} %collective-permute-done.1.refs_1_), custom_call_target="tpu_custom_call" | custom-call | tf_op jit(solution)/shard_map/prep_kv/pallas_call | solution.py:101
  4.0 1.9 %collective-permute-start.2 = (bf16[528,256]{1,0:T(8,128)(2,1)S(1)}, bf16[528,256]{1,0:T(8,128)(2,1)S(1)}, u32[]{:S(2)}, u32[]{:S(2)}) collective-permute-start(bf16[528,256]{1,0:T(8,128)(2,1)S(1)} %prep_kv.2), channel_id=1, source_target_pairs={{0,1},{1,0},{2,3},{3,2},{4,5},{5,4},{6,7},{7,6},{8,9},{9,8},{10,11... | collective-permute-start | bytes 811016 | tf_op jit(solution)/shard_map/ppermute | solution.py:32
  5.9 1.4 %prep_kv.3.lower_ref.refs_0_.refs_4_ = bf16[528,256]{1,0:T(8,128)(2,1)S(1)} custom-call(bf16[256,512]{1,0:T(8,128)(2,1)} %k_ref.3, bf16[256,512]{1,0:T(8,128)(2,1)} %v_ref.3, s32[1,2]{1,0:T(1,128)} %refs_0_.3), custom_call_target="tpu_custom_call" | custom-call | tf_op jit(solution)/shard_map/prep_kv/pallas_call | solution.py:101
  7.3 1.3 %collective-permute-start.6 = (bf16[528,256]{1,0:T(8,128)(2,1)S(1)}, bf16[528,256]{1,0:T(8,128)(2,1)S(1)}, u32[]{:S(2)}, u32[]{:S(2)}) collective-permute-start(bf16[528,256]{1,0:T(8,128)(2,1)S(1)} %prep_kv.3.lower_ref.refs_0_.refs_4_), channel_id=1, source_target_pairs={{0,4},{1,5},{2,6},{3,7},{4,8},{5,9},{6,10},{7,11},{8,12},{9,13},{1... | collective-permute-start | bytes 811016 | tf_op jit(solution)/shard_map/ppermute | solution.py:37
  8.6 1.2 %prep_q.3 = bf16[2,128,1024]{2,1,0:T(8,128)(2,1)S(1)} custom-call(bf16[256,2048]{1,0:T(8,128)(2,1)} %q_ref.3), custom_call_target="tpu_custom_call" | custom-call | tf_op jit(solution)/shard_map/prep_q/pallas_call | solution.py:141
  9.8 0.4 collective-permute-start
  10.2 5.1 %collective-permute-done.6.lower_ref.upper_ref.refs_0_.refs_6_ = bf16[528,256]{1,0:T(8,128)(2,1)S(1)} collective-permute-done((bf16[528,256]{1,0:T(8,128)(2,1)S(1)}, bf16[528,256]{1,0:T(8,128)(2,1)S(1)}, u32[]{:S(2)}, u32[]{:S(2)}) %collective-permute-start.6) | collective-permute-done | bytes 270368 | tf_op jit(solution)/shard_map/ppermute | solution.py:37
  15.3 1.3 %collective-permute-start.7 = (bf16[528,256]{1,0:T(8,128)(2,1)S(1)}, bf16[528,256]{1,0:T(8,128)(2,1)S(1)}, u32[]{:S(2)}, u32[]{:S(2)}) collective-permute-start(bf16[528,256]{1,0:T(8,128)(2,1)S(1)} %collective-permute-done.6.lower_ref.upper_ref.refs_0_.refs_6_), channel_id=1, source_target_pairs={{0,4},{1,5},{2,6},{3,7},{4,8},{5,9},{6,10},{7,11},{8,12},{9,13},{1... | collective-permute-start | bytes 811016 | tf_op jit(solution)/shard_map/ppermute | solution.py:37
  16.7 0.3 collective-permute-start.10
  17.0 4.2 %collective-permute-done.3.lower_ref.upper_ref.refs_1_.refs_2_ = bf16[528,256]{1,0:T(8,128)(2,1)S(1)} collective-permute-done((bf16[528,256]{1,0:T(8,128)(2,1)S(1)}, bf16[528,256]{1,0:T(8,128)(2,1)S(1)}, u32[]{:S(2)}, u32[]{:S(2)}) %collective-permute-start.3) | collective-permute-done | bytes 270368 | tf_op jit(solution)/shard_map/ppermute | solution.py:37
  21.1 1.3 %collective-permute-start.4 = (bf16[528,256]{1,0:T(8,128)(2,1)S(1)}, bf16[528,256]{1,0:T(8,128)(2,1)S(1)}, u32[]{:S(2)}, u32[]{:S(2)}) collective-permute-start(bf16[528,256]{1,0:T(8,128)(2,1)S(1)} %collective-permute-done.3.lower_ref.upper_ref.refs_1_.refs_2_), channel_id=1, source_target_pairs={{0,4},{1,5},{2,6},{3,7},{4,8},{5,9},{6,10},{7,11},{8,12},{9,13},{1... | collective-permute-start | bytes 811016 | tf_op jit(solution)/shard_map/ppermute | solution.py:37
  22.4 1.2 %prep_q.2.refs_2_.refs_3_.refs_0_ = bf16[2,128,1024]{2,1,0:T(8,128)(2,1)S(1)} custom-call(bf16[256,2048]{1,0:T(8,128)(2,1)} %q_ref.3), custom_call_target="tpu_custom_call" | custom-call | tf_op jit(solution)/shard_map/prep_q/pallas_call | solution.py:141
  23.6 3.3 %collective-permute-done.7.upper_ref.refs_0_.refs_5_ = bf16[528,256]{1,0:T(8,128)(2,1)S(1)} collective-permute-done((bf16[528,256]{1,0:T(8,128)(2,1)S(1)}, bf16[528,256]{1,0:T(8,128)(2,1)S(1)}, u32[]{:S(2)}, u32[]{:S(2)}) %collective-permute-start.7) | collective-permute-done | bytes 270368 | tf_op jit(solution)/shard_map/ppermute | solution.py:37
  27.3 1.3 %collective-permute-start.9 = (bf16[528,256]{1,0:T(8,128)(2,1)S(1)}, bf16[528,256]{1,0:T(8,128)(2,1)S(1)}, u32[]{:S(2)}, u32[]{:S(2)}) collective-permute-start(bf16[528,256]{1,0:T(8,128)(2,1)S(1)} %pick.6), channel_id=1, source_target_pairs={{0,2},{1,3},{2,0},{3,1},{4,6},{5,7},{6,4},{7,5},{8,10},{9,11},{10,... | collective-permute-start | bytes 811016 | tf_op jit(solution)/shard_map/ppermute | solution.py:32
  28.6 3.5 %attend.6 = (f32[2,2,128,1024]{3,2,1,0:T(8,128)S(1)}, f32[2,2,2,1,1024]{4,3,2,1,0:T(1,128)S(1)}, f32[4,1,128]{2,1,0:T(1,128)S(1)}) custom-call(bf16[528,256]{1,0:T(8,128)(2,1)S(1)} %prep_kv.3.lower_ref.refs_0_.refs_4_, bf16[528,256]{1,0:T(8,128)(2,1)S(1)} %collective-permute-done.2.lower_ref.refs_1_.refs_5_, ...), custom_call_target="tpu_custom_call" | custom-call | flops 1073741824 | bytes 6291456 | tf_op jit(solution)/shard_map/attend/pallas_call | solution.py:428
  32.1 4.8 %attend.7 = (f32[2,2,128,1024]{3,2,1,0:T(8,128)S(1)}, f32[2,2,2,1,1024]{4,3,2,1,0:T(1,128)S(1)}, f32[4,1,128]{2,1,0:T(1,128)S(1)}) custom-call(bf16[528,256]{1,0:T(8,128)(2,1)S(1)} %collective-permute-done.6.lower_ref.upper_ref.refs_0_.refs_6_, ...), custom_call_target="tpu_custom_call", output_to_operand_aliasing={{0}: (7, {}), {1}: (8, {}), {2}: (9, {})} | custom-call | flops 1073741824 | bytes 6291456 | tf_op jit(solution)/shard_map/attend/pallas_call | solution.py:428
  37.0 0.5 collective-permute-start.5
  37.6 5.9 %attend.8 = (f32[2,2,128,1024]{3,2,1,0:T(8,128)S(1)}, f32[2,2,2,1,1024]{4,3,2,1,0:T(1,128)S(1)}, f32[4,1,128]{2,1,0:T(1,128)S(1)}) custom-call(bf16[2,128,1024]{2,1,0:T(8,128)(2,1)S(1)} %prep_q.2.refs_2_.refs_3_.refs_0_, ...), custom_call_target="tpu_custom_call", output_to_operand_aliasing={{0}: (4, {}), {1}: (5, {}), {2}: (6, {})} | custom-call | flops 1073741824 | bytes 6291456 | tf_op jit(solution)/shard_map/attend/pallas_call | solution.py:428
  43.5 3.3 %attend.9 = (f32[2,2,128,1024]{3,2,1,0:T(8,128)S(1)}, f32[2,2,2,1,1024]{4,3,2,1,0:T(1,128)S(1)}, f32[4,1,128]{2,1,0:T(1,128)S(1)}) custom-call(bf16[2,128,1024]{2,1,0:T(8,128)(2,1)S(1)} %prep_q.2.refs_2_.refs_3_.refs_0_, ...), custom_call_target="tpu_custom_call", output_to_operand_aliasing={{0}: (3, {}), {1}: (4, {}), {2}: (5, {})} | custom-call | flops 536870912 | bytes 6291456 | tf_op jit(solution)/shard_map/attend/pallas_call | solution.py:428
  46.8 4.9 %attend.10 = (bf16[256,2048]{1,0:T(8,128)(2,1)}, bf16[256,1024]{1,0:T(8,128)(2,1)S(1)}, f32[2,2,128,1024]{3,2,1,0:T(8,128)S(1)}, f32[2,2,2,1,1024]{4,3,2,1,0:T(1,128)S(1)}, f32[4,1,128]{2,1,0:T(1,128)S(1)}) custom-call(bf16[528,256]{1,0:T(8,128)(2,1)S(1)} %collective-permute-done.7.upper_ref.refs_0_.refs_, ...), custom_call_target="tpu_custom_call", output_to_operand_aliasing={{2}: (8, {}), {3}: (9, {}), {4}: (10, {})} | custom-call | flops 1610612736 | bytes 6291456 | tf_op jit(solution)/shard_map/attend/pallas_call | solution.py:428
  51.9 1.7 %collective-permute-start.11 = (bf16[256,1024]{1,0:T(8,128)(2,1)S(1)}, bf16[256,1024]{1,0:T(8,128)(2,1)S(1)}, u32[]{:S(2)}, u32[]{:S(2)}) collective-permute-start(bf16[256,1024]{1,0:T(8,128)(2,1)S(1)} %get-tuple-element.41), channel_id=1, source_target_pairs={{0,1},{1,0},{2,3},{3,2},{4,5},{5,4},{6,7},{7,6},{8,9},{9,8},{10,11... | collective-permute-start | bytes 1572872 | tf_op jit(solution)/shard_map/ppermute | solution.py:32
  53.6 1.5 %collective-permute-done.11.got_ref = bf16[256,1024]{1,0:T(8,128)(2,1)S(1)} collective-permute-done((bf16[256,1024]{1,0:T(8,128)(2,1)S(1)}, bf16[256,1024]{1,0:T(8,128)(2,1)S(1)}, u32[]{:S(2)}, u32[]{:S(2)}) %collective-permute-start.11) | collective-permute-done | bytes 524320 | tf_op jit(solution)/shard_map/ppermute | solution.py:32
  55.1 0.8 %merge.1 = bf16[256,2048]{1,0:T(8,128)(2,1)} custom-call(bf16[256,1024]{1,0:T(8,128)(2,1)S(1)} %collective-permute-done.11.got_ref, bf16[256,2048]{1,0:T(8,128)(2,1)} %get-tuple-element.42.full_in), custom_call_target="tpu_custom_call", output_to_operand_aliasing={{}: (1, {})} | custom-call | tf_op jit(solution)/shard_map/merge/pallas_call | solution.py:189
  (15 shorter events, 0.9 us)
Async XLA Ops:
  0.0 2.6 %collective-permute-start.1 = (s32[1,2]{1,0:T(1,128)}, s32[1,2]{1,0:T(1,128)S(1)}, u32[]{:S(2)}, u32[]{:S(2)}) collective-permute-start(s32[1,2]{1,0:T(1,128)} %refs_0_.3), channel_id=1, source_target_pairs={{0,2},{1,3},{2,0},{3,1},{4,6},{5,7},{6,4},{7,5},{8,10},{9,11},{10,... | collective-permute-start | bytes 32 | tf_op jit(solution)/shard_map/ppermute | solution.py:32
  4.0 6.2 %collective-permute-start.2 = (bf16[528,256]{1,0:T(8,128)(2,1)S(1)}, bf16[528,256]{1,0:T(8,128)(2,1)S(1)}, u32[]{:S(2)}, u32[]{:S(2)}) collective-permute-start(bf16[528,256]{1,0:T(8,128)(2,1)S(1)} %prep_kv.2), channel_id=1, source_target_pairs={{0,1},{1,0},{2,3},{3,2},{4,5},{5,4},{6,7},{7,6},{8,9},{9,8},{10,11... | collective-permute-start | bytes 811016 | tf_op jit(solution)/shard_map/ppermute | solution.py:32
  7.3 8.1 %collective-permute-start.6 = (bf16[528,256]{1,0:T(8,128)(2,1)S(1)}, bf16[528,256]{1,0:T(8,128)(2,1)S(1)}, u32[]{:S(2)}, u32[]{:S(2)}) collective-permute-start(bf16[528,256]{1,0:T(8,128)(2,1)S(1)} %prep_kv.3.lower_ref.refs_0_.refs_4_), channel_id=1, source_target_pairs={{0,4},{1,5},{2,6},{3,7},{4,8},{5,9},{6,10},{7,11},{8,12},{9,13},{1... | collective-permute-start | bytes 811016 | tf_op jit(solution)/shard_map/ppermute | solution.py:37
  9.8 18.8 %collective-permute-start = (bf16[2,128,1024]{2,1,0:T(8,128)(2,1)S(1)}, bf16[2,128,1024]{2,1,0:T(8,128)(2,1)S(1)}, u32[]{:S(2)}, u32[]{:S(2)}) collective-permute-start(bf16[2,128,1024]{2,1,0:T(8,128)(2,1)S(1)} %prep_q.3), channel_id=1, source_target_pairs={{0,1},{1,0},{2,3},{3,2},{4,5},{5,4},{6,7},{7,6},{8,9},{9,8},{10,11... | collective-permute-start | bytes 1572872 | tf_op jit(solution)/shard_map/ppermute | solution.py:32
  10.2 10.9 %collective-permute-start.3 = (bf16[528,256]{1,0:T(8,128)(2,1)S(1)}, bf16[528,256]{1,0:T(8,128)(2,1)S(1)}, u32[]{:S(2)}, u32[]{:S(2)}) collective-permute-start(bf16[528,256]{1,0:T(8,128)(2,1)S(1)} %collective-permute-done.2.lower_ref.refs_1_.refs_5_), channel_id=1, source_target_pairs={{0,4},{1,5},{2,6},{3,7},{4,8},{5,9},{6,10},{7,11},{8,12},{9,13},{1... | collective-permute-start | bytes 811016 | tf_op jit(solution)/shard_map/ppermute | solution.py:37
  15.3 11.6 %collective-permute-start.7 = (bf16[528,256]{1,0:T(8,128)(2,1)S(1)}, bf16[528,256]{1,0:T(8,128)(2,1)S(1)}, u32[]{:S(2)}, u32[]{:S(2)}) collective-permute-start(bf16[528,256]{1,0:T(8,128)(2,1)S(1)} %collective-permute-done.6.lower_ref.upper_ref.refs_0_.refs_6_), channel_id=1, source_target_pairs={{0,4},{1,5},{2,6},{3,7},{4,8},{5,9},{6,10},{7,11},{8,12},{9,13},{1... | collective-permute-start | bytes 811016 | tf_op jit(solution)/shard_map/ppermute | solution.py:37
  16.7 15.4 %collective-permute-start.10 = (bf16[528,256]{1,0:T(8,128)(2,1)S(1)}, bf16[528,256]{1,0:T(8,128)(2,1)S(1)}, u32[]{:S(2)}, u32[]{:S(2)}) collective-permute-start(bf16[528,256]{1,0:T(8,128)(2,1)S(1)} %pick.7), channel_id=1, source_target_pairs={{0,2},{1,3},{2,0},{3,1},{4,6},{5,7},{6,4},{7,5},{8,10},{9,11},{10,... | collective-permute-start | bytes 811016 | tf_op jit(solution)/shard_map/ppermute | solution.py:32
  21.1 15.8 %collective-permute-start.4 = (bf16[528,256]{1,0:T(8,128)(2,1)S(1)}, bf16[528,256]{1,0:T(8,128)(2,1)S(1)}, u32[]{:S(2)}, u32[]{:S(2)}) collective-permute-start(bf16[528,256]{1,0:T(8,128)(2,1)S(1)} %collective-permute-done.3.lower_ref.upper_ref.refs_1_.refs_2_), channel_id=1, source_target_pairs={{0,4},{1,5},{2,6},{3,7},{4,8},{5,9},{6,10},{7,11},{8,12},{9,13},{1... | collective-permute-start | bytes 811016 | tf_op jit(solution)/shard_map/ppermute | solution.py:37
  27.0 19.8 %collective-permute-start.8 = (bf16[528,256]{1,0:T(8,128)(2,1)S(1)}, bf16[528,256]{1,0:T(8,128)(2,1)S(1)}, u32[]{:S(2)}, u32[]{:S(2)}) collective-permute-start(bf16[528,256]{1,0:T(8,128)(2,1)S(1)} %pick.5), channel_id=1, source_target_pairs={{0,2},{1,3},{2,0},{3,1},{4,6},{5,7},{6,4},{7,5},{8,10},{9,11},{10,... | collective-permute-start | bytes 811016 | tf_op jit(solution)/shard_map/ppermute | solution.py:32
  27.3 16.2 %collective-permute-start.9 = (bf16[528,256]{1,0:T(8,128)(2,1)S(1)}, bf16[528,256]{1,0:T(8,128)(2,1)S(1)}, u32[]{:S(2)}, u32[]{:S(2)}) collective-permute-start(bf16[528,256]{1,0:T(8,128)(2,1)S(1)} %pick.6), channel_id=1, source_target_pairs={{0,2},{1,3},{2,0},{3,1},{4,6},{5,7},{6,4},{7,5},{8,10},{9,11},{10,... | collective-permute-start | bytes 811016 | tf_op jit(solution)/shard_map/ppermute | solution.py:32
  37.0 14.7 %collective-permute-start.5 = (bf16[528,256]{1,0:T(8,128)(2,1)S(1)}, bf16[528,256]{1,0:T(8,128)(2,1)S(1)}, u32[]{:S(2)}, u32[]{:S(2)}) collective-permute-start(bf16[528,256]{1,0:T(8,128)(2,1)S(1)} %pick.4), channel_id=1, source_target_pairs={{0,2},{1,3},{2,0},{3,1},{4,6},{5,7},{6,4},{7,5},{8,10},{9,11},{10,... | collective-permute-start | bytes 811016 | tf_op jit(solution)/shard_map/ppermute | solution.py:32
  51.9 3.2 %collective-permute-start.11 = (bf16[256,1024]{1,0:T(8,128)(2,1)S(1)}, bf16[256,1024]{1,0:T(8,128)(2,1)S(1)}, u32[]{:S(2)}, u32[]{:S(2)}) collective-permute-start(bf16[256,1024]{1,0:T(8,128)(2,1)S(1)} %get-tuple-element.41), channel_id=1, source_target_pairs={{0,1},{1,0},{2,3},{3,2},{4,5},{5,4},{6,7},{7,6},{8,9},{9,8},{10,11... | collective-permute-start | bytes 1572872 | tf_op jit(solution)/shard_map/ppermute | solution.py:32
